TPU v7x, 32 devices: a whole 2x2x4 slice. The times are simulated.
32 devices in a mesh: hel: 4 (over z), rad: 8 (over y, x, core).
Axes of the slice: x: 2, y: 2, z: 4, core: 2. Of those that a mesh axis runs over, the one named last changes fastest.
Arguments:
- packet: float32 [2, 8, 1024, 8, 1024], P(None, 'hel', 'rad'), may hold values from -6 to 6
- radial_weight: float32 [8, 1024], P(None, 'rad'), may hold values from 0.25 to 1.75
- tile_blocks: float32 [24, 128, 128], replicated, may hold values from -0.1875 to 0.1875
- tile_list: int32 [24, 3], replicated, may hold values from 0 to 7, as said below
- coupling: float32 [8, 1024], replicated, may hold values from 0.1 to 0.5
Outputs:
- advanced: float32 [2, 8, 1024, 8, 1024], P(None, 'hel', 'rad')
Inputs may be any that keep to these rules, and one draw needn't show every extreme that they name: `tile_list`: each row is (block row, block column, radial weight index): block indices lie below 8 and weight indices below 8; every block row and every weight index occurs in some row; rows may repeat pairs.
All inputs are finite; a program needn't handle non-finite values.
Results may differ from a plain program's by a relative error of at most 0.0001.
Values sent between devices are 32-bit elements; how exact they have to be, the bound alone decides.
No kernel may reach another device: no remote copies, remote signals or barrier semaphores. Data moves between devices by JAX's collectives and lax.ppermute only.
A program may use at most 256 MiB of HBM per device.

v0:
```python
import functools

import jax
import jax.numpy as jnp
import numpy as np
from jax import lax
from jax.experimental import pallas as pl
from jax.experimental.pallas import tpu as pltpu
from jax.sharding import PartitionSpec as P


R = 1024
TILE = 128
TAYLOR = 3
CHUNKS = (2, 1, 2, 2, 1)
EARLY = (4,)
PLAN = (
    ("F", 0), ("F", 1), ("K", 0), ("B", 0), ("K", 1), ("B", 1), ("E", 0), ("F", 2), ("E", 1),
    ("T", 0), ("K", 2), ("B", 2), ("T", 1), ("T", 0), ("F", 3), ("E", 2), ("T", 1), ("F", 4),
    ("K", 3), ("B", 3), ("T", 2), ("T", 1), ("K", 4), ("B", 4), ("E", 3), ("T", 2), ("G", 4),
    ("T", 3), ("L", 4), ("C", 4), ("T", 0), ("T", 2), ("T", 4), ("T", 3), ("T", 4), ("T", 3),
    ("T", 4),
)


kinetic_scale = 0.5


def extended(block, sides, width):
    for axis, dim in sides:
        count = lax.axis_size(axis)
        forward = [(i, i + 1) for i in range(count - 1)]
        backward = [(target, source) for source, target in forward]
        low = lax.ppermute(
            lax.slice_in_dim(block, block.shape[dim] - width, None, axis=dim), axis, forward
        )
        high = lax.ppermute(lax.slice_in_dim(block, 0, width, axis=dim), axis, backward)
        block = jnp.concatenate([low, block, high], axis=dim)
    return block


def potential(term, radial_weight, tile_blocks, tile_list):
    term_shape = term.shape
    blocks = term.reshape(
        term_shape[0], term_shape[1], term_shape[2], term_shape[3], term_shape[4] // TILE, TILE
    )

    def add_tile(position, summed):
        target = tile_list[position, 0]
        source = tile_list[position, 1]
        weight_row = tile_list[position, 2]
        source_block = lax.dynamic_index_in_dim(blocks, source, 4, keepdims=False)
        matrix = lax.dynamic_index_in_dim(tile_blocks, position, 0, keepdims=False)
        product = jnp.einsum(
            "ckrvi,ij->ckrvj", source_block, matrix, precision=lax.Precision.HIGHEST
        )
        factor = lax.dynamic_index_in_dim(radial_weight, weight_row, 0, keepdims=False)
        product = product * factor[None, None, :, None, None]
        current = lax.dynamic_index_in_dim(summed, target, 4, keepdims=False)
        return lax.dynamic_update_index_in_dim(summed, current + product, target, 4)

    summed = lax.fori_loop(0, tile_list.shape[0], add_tile, jnp.zeros(blocks.shape, jnp.float32))
    return summed.reshape(term_shape)


def coupling_window(coupling, helices):
    first_helix = lax.axis_index("hel") * helices
    coupled = jnp.concatenate([jnp.zeros((1, coupling.shape[1]), jnp.float32), coupling], axis=0)
    return lax.dynamic_slice_in_dim(coupled, first_helix, helices + 1, 0)


def coriolis_rim(term, coupling, radial_factor):
    helices = term.shape[1]
    padded = extended(term, (("hel", 1),), 1)
    window = coupling_window(coupling, helices)
    lower = window[:helices]
    upper = window[1:]
    mixed = (
        upper[None, :, None, None, :] * padded[:, 2:]
        + lower[None, :, None, None, :] * padded[:, :-2]
    )
    return mixed * radial_factor[None, None, :, None, None]


def transform(matrix, moving):
    return jnp.einsum("qr,cnrm->cnqm", matrix, moving, precision=lax.Precision.HIGHEST)


def propagate(moving, cosine_table, sine_table, phase_cos, phase_sin):
    length = moving.shape[2]
    cos_part = transform(cosine_table, moving)
    sin_part = transform(sine_table, moving)
    spec_real = cos_part[0] + sin_part[1]
    spec_imag = cos_part[1] - sin_part[0]
    turn_cos = phase_cos[None, :, None]
    turn_sin = phase_sin[None, :, None]
    turned = jnp.stack(
        [turn_cos * spec_real + turn_sin * spec_imag, turn_cos * spec_imag - turn_sin * spec_real]
    )
    cos_back = transform(cosine_table, turned)
    sin_back = transform(sine_table, turned)
    return jnp.stack([(cos_back[0] - sin_back[1]) / length, (cos_back[1] + sin_back[0]) / length])


def expand(current, radial_weight, tile_blocks, tile_list, coupling, radial_factor, coriolis):
    advanced = current
    for degree in range(1, TAYLOR + 1):
        applied = potential(current, radial_weight, tile_blocks, tile_list) + coriolis(
            current, coupling, radial_factor
        )
        current = jnp.stack([applied[1], -applied[0]]) / degree
        advanced = advanced + current
    return advanced


def radial_factor_of(radial):
    distance = (lax.axis_index("rad") * radial + jnp.arange(radial, dtype=jnp.int32)).astype(
        jnp.float32
    )
    return 1.0 / (1.0 + 3.0 * distance / R) ** 2


def body_any(packet, radial_weight, tile_blocks, tile_list, coupling):
    two_parts, helices, radial, vibration, channels = packet.shape
    wave_index = jnp.arange(R, dtype=jnp.int32)
    angle_table = (wave_index[:, None] * wave_index[None, :] % R).astype(jnp.float32) * (
        2.0 * jnp.pi / R
    )
    cosine_table = jnp.cos(angle_table)
    sine_table = jnp.sin(angle_table)
    signed = jnp.where(wave_index < R // 2, wave_index, wave_index - R).astype(jnp.float32)
    phase_angle = kinetic_scale * (2.0 * jnp.pi * signed / R) ** 2
    phase_cos = jnp.cos(phase_angle)
    phase_sin = jnp.sin(phase_angle)
    flattened = packet.reshape(two_parts, helices, radial, vibration * channels)
    moved = propagate(
        lax.all_to_all(flattened, "rad", split_axis=3, concat_axis=2, tiled=True),
        cosine_table,
        sine_table,
        phase_cos,
        phase_sin,
    )
    returned = lax.all_to_all(moved, "rad", split_axis=2, concat_axis=3, tiled=True)
    current = returned.reshape(packet.shape)
    return expand(
        current,
        radial_weight,
        tile_blocks,
        tile_list,
        coupling,
        radial_factor_of(radial),
        coriolis_rim,
    )


VMEM_LIMIT = 60 * 1024 * 1024


def params(axes):
    return pltpu.CompilerParams(
        dimension_semantics=("arbitrary",) * axes, vmem_limit_bytes=VMEM_LIMIT
    )


def split_two(value):
    high = value.astype(jnp.bfloat16)
    low = (value - high.astype(jnp.float32)).astype(jnp.bfloat16)
    return high, low


def propagator_column(length):
    wave = np.arange(length)
    signed = np.where(wave < length // 2, wave, wave - length).astype(np.float64)
    phase = kinetic_scale * (2.0 * np.pi * signed / length) ** 2
    column = np.fft.ifft(np.exp(-1j * phase))
    return column.real.astype(np.float32), column.imag.astype(np.float32)


STRIPE = 16
ROWS = 64
UNROLL = 8


def circulant_kernel(real_ref, imag_ref, high_ref, low_ref):
    rows = high_ref.shape[2]
    first = pl.program_id(0) * rows
    for part, ref in ((0, real_ref), (1, imag_ref)):
        stripe = jnp.broadcast_to(ref[...], (STRIPE, ref.shape[1]))
        row = lax.broadcasted_iota(jnp.int32, stripe.shape, 0)
        step = 1
        while step < STRIPE:
            stripe = jnp.where(row // step % 2 == 1, pltpu.roll(stripe, step, 1), stripe)
            step *= 2

        @pl.loop(0, rows // STRIPE)
        def _(j):
            at = pl.multiple_of(j * STRIPE, STRIPE)
            high, low = split_two(pltpu.roll(stripe, first + at, 1))
            high_ref[0, part, pl.ds(at, STRIPE)] = high
            low_ref[0, part, pl.ds(at, STRIPE)] = low


def circulant(length, rows):
    real, imag = propagator_column(length)
    grid = length // rows
    spec = pl.BlockSpec((1, 2, rows, length), lambda m: (m, 0, 0, 0))
    line = pl.BlockSpec((1, length), lambda m: (0, 0))
    shape = jax.ShapeDtypeStruct((grid, 2, rows, length), jnp.bfloat16)
    return pl.pallas_call(
        circulant_kernel,
        grid=(grid,),
        in_specs=[line, line],
        out_specs=[spec, spec],
        out_shape=[shape, shape],
        compiler_params=params(1),
        name="circulant",
    )(jnp.asarray(real)[None], jnp.asarray(imag)[None])


def kinetic_kernel(*refs):
    moving_ref, high_ref, low_ref, out_ref, xh_ref, xl_ref = refs[-6:]
    sources, _, _, _, radial, lanes = moving_ref.shape
    length = sources * radial
    for part in range(2):
        value = moving_ref[:, 0, 0, part].reshape(length, lanes)
        high, low = split_two(value)
        xh_ref[:, part * lanes : (part + 1) * lanes] = high
        xl_ref[:, part * lanes : (part + 1) * lanes] = low
    groups, _, rows, _ = high_ref.shape
    per = rows // radial

    @pl.loop(0, groups, unroll=2)
    def _(m):
        left = high_ref[m].reshape(2 * rows, length)
        small = low_ref[m].reshape(2 * rows, length)
        dot = functools.partial(jnp.dot, preferred_element_type=jnp.float32)
        high = xh_ref[...]
        total = dot(left, high) + (dot(left, xl_ref[...]) + dot(small, high))
        real = total[:rows, :lanes] - total[rows:, lanes:]
        imag = total[:rows, lanes:] + total[rows:, :lanes]
        for j in range(per):
            out_ref[m * per + j, 0, 0, 0] = real[j * radial : (j + 1) * radial]
            out_ref[m * per + j, 0, 0, 1] = imag[j * radial : (j + 1) * radial]


def kinetic(moving, high, low, afters):
    blocks, helices, count, _, radial, lanes = moving.shape
    block = pl.BlockSpec((blocks, 1, 1, 2, radial, lanes), lambda k, v: (0, k, v, 0, 0, 0))
    whole = pl.BlockSpec(high.shape, lambda k, v: (0, 0, 0, 0), pipeline_mode=pl.Buffered(1))
    length = blocks * radial
    return pl.pallas_call(
        kinetic_kernel,
        grid=(helices, count),
        in_specs=[*[ANYWHERE] * len(afters), block, whole, whole],
        out_specs=block,
        out_shape=jax.ShapeDtypeStruct(moving.shape, jnp.float32),
        scratch_shapes=[
            pltpu.VMEM((length, 2 * lanes), jnp.bfloat16),
            pltpu.VMEM((length, 2 * lanes), jnp.bfloat16),
        ],
        compiler_params=params(2),
        cost_estimate=pl.CostEstimate(
            flops=2 * 3 * helices * count * 4 * length * length * lanes,
            bytes_accessed=8 * moving.size + 8 * length * length,
            transcendentals=0,
        ),
        name="kinetic",
    )(*afters, moving, high, low)


def places():
    return [(c, i) for c, count in enumerate(CHUNKS) for i in range(count)]


def pack_kernel(chunks, packet_ref, *chunk_refs):
    @pl.loop(0, packet_ref.shape[4] // TILE)
    def _(b):
        lanes = pl.ds(pl.multiple_of(b * TILE, TILE), TILE)
        turned = jnp.swapaxes(packet_ref[0, 0, :, :, lanes], 0, 1)
        for v, (c, i) in enumerate(places()):
            if c in chunks:
                chunk_refs[chunks.index(c)][b, 0, i, 0] = turned[v]


def pack(packet, chunks):
    parts, helices, radial, vibration, channels = packet.shape
    blocks = channels // TILE
    counts = [CHUNKS[c] for c in chunks]
    share = sum(counts) / vibration
    return pl.pallas_call(
        functools.partial(pack_kernel, chunks),
        grid=(helices, parts),
        in_specs=[
            pl.BlockSpec((1, 1, radial, vibration, channels), lambda k, p: (p, k, 0, 0, 0))
        ],
        out_specs=[
            pl.BlockSpec((blocks, 1, count, 1, radial, TILE), lambda k, p: (0, k, 0, p, 0, 0))
            for count in counts
        ],
        out_shape=[
            jax.ShapeDtypeStruct((blocks, helices, count, parts, radial, TILE), jnp.float32)
            for count in counts
        ],
        compiler_params=params(2),
        cost_estimate=pl.CostEstimate(
            flops=0, bytes_accessed=int(4 * packet.size * (1 + share)), transcendentals=0
        ),
        name="pack",
    )(packet)


def unpack_kernel(*refs):
    out_ref = refs[-1]

    @pl.loop(0, out_ref.shape[4] // TILE)
    def _(b):
        lanes = pl.ds(pl.multiple_of(b * TILE, TILE), TILE)
        lines = [refs[c][0, b, i, 0] for c, i in places()]
        out_ref[0, 0, :, :, lanes] = jnp.swapaxes(jnp.stack(lines), 0, 1)


def unpack(chunks, packet_shape):
    parts, helices, radial, vibration, channels = packet_shape
    blocks = channels // TILE
    return pl.pallas_call(
        unpack_kernel,
        grid=(helices, parts),
        in_specs=[
            pl.BlockSpec((1, blocks, count, 1, radial, TILE), lambda k, p: (k, 0, 0, p, 0, 0))
            for count in CHUNKS
        ],
        out_specs=pl.BlockSpec(
            (1, 1, radial, vibration, channels), lambda k, p: (p, k, 0, 0, 0)
        ),
        out_shape=jax.ShapeDtypeStruct(packet_shape, jnp.float32),
        compiler_params=params(2),
        name="unpack",
    )(*chunks)


def gate_kernel(*refs):
    del refs


ANYWHERE = pl.BlockSpec(memory_space=pl.ANY)


def gate(value, *afters):
    return pl.pallas_call(
        gate_kernel,
        in_specs=[ANYWHERE] * (1 + len(afters)),
        out_specs=ANYWHERE,
        out_shape=jax.ShapeDtypeStruct(value.shape, value.dtype),
        input_output_aliases={0: 0},
        compiler_params=params(0),
        name="gate",
    )(value, *afters)


def taylor_kernel(degree, helices, skipped, sums_in, last, list_ref, *refs):
    refs = list(refs)[skipped:]
    term_refs = [refs.pop(0) for _ in range(helices)]
    low_ref, high_ref, tile_ref, weight_ref, window_ref, factor_ref = (
        refs.pop(0) for _ in range(6)
    )
    sum_refs = [refs.pop(0) for _ in range(helices)] if sums_in else []
    next_refs = None if last else [refs.pop(0) for _ in range(helices)]
    total_refs = [refs.pop(0) for _ in range(helices)] if sums_in and not last else None
    out_ref = refs.pop(0) if last else None
    split_ref, summed_ref = refs
    term_refs, sum_refs, (low_ref, high_ref) = (
        [r.at[:, 0] if len(r.shape) == 6 else r for r in some]
        for some in (term_refs, sum_refs, (low_ref, high_ref))
    )
    blocks, _, _, radial, lanes = term_refs[0].shape
    rows = helices * 2 * radial
    factor = factor_ref[...]

    @pl.loop(0, blocks)
    def _(b):
        for k in range(helices):
            below = low_ref if k == 0 else term_refs[k - 1]
            above = high_ref if k == helices - 1 else term_refs[k + 1]
            lower = window_ref[k, b]
            upper = window_ref[k + 1, b]
            for part in range(2):
                at = (k * 2 + part) * radial
                high, low = split_two(term_refs[k][b, 0, part])
                split_ref[b, at : at + radial, :lanes] = high
                split_ref[b, at : at + radial, lanes:] = low
                mixed = upper * above[b, 0, part] + lower * below[b, 0, part]
                summed_ref[b, at : at + radial] = mixed * factor

    def add_tile(t, carry):
        target = list_ref[t, 0]
        source = list_ref[t, 1]
        weight = weight_ref[list_ref[t, 2]]
        both = jnp.dot(split_ref[source], tile_ref[t], preferred_element_type=jnp.float32)
        for i in range(rows // radial):
            at = i * radial
            product = both[at : at + radial, :lanes] + both[at : at + radial, lanes:]
            summed_ref[target, at : at + radial] += product * weight
        return carry

    lax.fori_loop(0, tile_ref.shape[0], add_tile, 0, unroll=UNROLL)

    scale = 1.0 / degree

    @pl.loop(0, blocks)
    def _(b):
        for k in range(helices):
            at = k * 2 * radial
            real = summed_ref[b, at + radial : at + 2 * radial] * scale
            imag = summed_ref[b, at : at + radial] * (-scale)
            for part, value in ((0, real), (1, imag)):
                if not last:
                    next_refs[k][b, 0, part] = value
                if not sums_in:
                    continue
                value = sum_refs[k][b, 0, part] + value
                if not last:
                    value = term_refs[k][b, 0, part] + value
                    total_refs[k][b, 0, part] = value
                else:
                    out_ref[k, b, 0, part] = value


def taylor(degree, terms, halo, sums, tile_list, tiles, weights, window, factor, afters):
    helices = window.shape[0] - 1
    last = degree == TAYLOR
    shape = (halo.shape[0], *halo.shape[2:]) if isinstance(halo, jax.Array) else halo[0].shape
    blocks, count, parts, radial, lanes = shape
    block = pl.BlockSpec((blocks, 1, parts, ROWS, lanes), lambda v, j, lists: (0, v, 0, j, 0))

    def whole(array):
        zeros = (0,) * array.ndim
        return pl.BlockSpec(
            array.shape, lambda v, j, lists: zeros, pipeline_mode=pl.Buffered(1)
        )

    def helix(k):
        return pl.BlockSpec(
            (blocks, 1, 1, parts, ROWS, lanes), lambda v, j, lists: (0, k, v, 0, j, 0)
        )

    def per_helix(fields):
        if isinstance(fields, (list, tuple)):
            return list(fields), [block] * len(fields)
        held = fields.shape[1]
        return [fields] * held, [helix(k) for k in range(held)]

    own, own_specs = per_helix(terms)
    sides, side_specs = per_helix(halo)
    operands = [*afters, *own, *sides, tiles, weights, window, factor]
    specs = [*[ANYWHERE] * len(afters), *own_specs, *side_specs]
    specs += [
        whole(tiles),
        pl.BlockSpec((weights.shape[0], ROWS, lanes), lambda v, j, lists: (0, j, 0)),
        whole(window),
        pl.BlockSpec((ROWS, lanes), lambda v, j, lists: (j, 0)),
    ]
    if sums is not None:
        summed, summed_specs = per_helix(sums)
        operands += summed
        specs += summed_specs
    field = jax.ShapeDtypeStruct(shape, jnp.float32)
    if last:
        shapes = [jax.ShapeDtypeStruct((helices, *shape), jnp.float32)]
        out_specs = [
            pl.BlockSpec(
                (helices, blocks, 1, parts, ROWS, lanes),
                lambda v, j, lists: (0, 0, v, 0, j, 0),
            )
        ]
    else:
        written = helices if sums is None else 2 * helices
        shapes = [field] * written
        out_specs = [block] * written
    rows = helices * parts * ROWS
    results = pl.pallas_call(
        functools.partial(
            taylor_kernel, degree, helices, len(afters), sums is not None, last
        ),
        grid_spec=pltpu.PrefetchScalarGridSpec(
            num_scalar_prefetch=1,
            grid=(count, radial // ROWS),
            in_specs=specs,
            out_specs=out_specs,
            scratch_shapes=[
                pltpu.VMEM((blocks, rows, 2 * lanes), jnp.bfloat16),
                pltpu.VMEM((blocks, rows, lanes), jnp.float32),
            ],
        ),
        out_shape=shapes,
        compiler_params=params(2),
        cost_estimate=pl.CostEstimate(
            flops=2 * 4 * count * helices * parts * radial * lanes * lanes * tiles.shape[0],
            bytes_accessed=4 * blocks * count * parts * radial * lanes * (helices + 2 + 2 * helices),
            transcendentals=0,
        ),
    )(tile_list, *operands)
    if last:
        return results[0], None
    return results[:helices], terms if sums is None else results[helices:]


def body_blocks(packet, radial_weight, tile_blocks, tile_list, coupling):
    _, helices, radial, _, channels = packet.shape
    blocks = channels // TILE
    count = lax.axis_size("hel")
    forward = [(i, i + 1) for i in range(count - 1)]
    backward = [(target, source) for source, target in forward]
    exchange = functools.partial(
        lax.all_to_all, axis_name="rad", split_axis=0, concat_axis=0, tiled=True
    )

    length = blocks * radial
    packed = pack(packet, [0])
    packed += pack(packet, list(range(1, len(CHUNKS))))
    high, low = circulant(length, 2 * radial)
    tile_high = lax.reduce_precision(tile_blocks, 8, 7)
    tile_low = (tile_blocks - tile_high).astype(jnp.bfloat16)
    tile_high = tile_high.astype(jnp.bfloat16)
    pair = jnp.concatenate([tile_high, tile_low], axis=2)
    tiles = jnp.concatenate([pair, pair], axis=1)
    weights = jnp.broadcast_to(radial_weight[:, :, None], (*radial_weight.shape, TILE))
    window = coupling_window(coupling, helices).reshape(helices + 1, blocks, 1, TILE)
    factor = jnp.broadcast_to(radial_factor_of(radial)[:, None], (radial, TILE))

    spectra, terms, halos, sums, degrees = {}, {}, {}, {}, {}
    previous, latest = (), ()

    def send(value):
        nonlocal previous, latest
        afters = [a for a in (*previous, *latest) if a is not value]
        if afters:
            value = gate(value, *afters)
            latest = (value,)
        previous = (exchange(value),)
        return previous[0]

    def halo(c, degree, first, last):
        degrees[c] = degree
        below = lax.ppermute(last, "hel", forward)
        halos[c] = below, lax.ppermute(first, "hel", backward)

    for c in EARLY:
        halo(c, 0, packed[c][:, 0], packed[c][:, -1])

    def run(kind, c):
        nonlocal latest
        if kind == "F":
            spectra[c] = send(packed[c])
        elif kind == "K":
            spectra[c] = kinetic(spectra[c], high, low, latest)
            latest = (spectra[c],)
        elif kind == "B":
            terms[c] = send(spectra[c])
        elif kind == "G":
            halos[c] = send(jnp.stack(halos[c], axis=1))
        elif kind == "L":
            halos[c] = kinetic(halos[c], high, low, latest)
            latest = (halos[c],)
        elif kind == "C":
            halos[c] = send(halos[c])
            degrees[c] = 1
        elif kind == "T":
            degree = degrees[c]
            terms[c], sums[c] = taylor(
                degree,
                terms[c],
                halos[c],
                sums.get(c),
                tile_list,
                tiles,
                weights,
                window,
                factor,
                latest,
            )
            latest = (terms[c],) if degree == TAYLOR else (terms[c][0],)

    for kind, c in PLAN:
        run(kind, c)
        if kind == "E":
            latest = terms[c][:, 0], terms[c][:, -1]
            halo(c, 1, *latest)
        elif kind == "T" and degrees[c] < TAYLOR:
            halo(c, degrees[c] + 1, terms[c][0], terms[c][-1])
    return unpack([terms[c] for c in range(len(CHUNKS))], packet.shape)


def solution(mesh):
    in_specs = (P(None, "hel", "rad", None, None), P(None, "rad"), P(), P(), P())
    out_specs = P(None, "hel", "rad", None, None)

    def sharded(body):
        return jax.shard_map(
            body, mesh=mesh, in_specs=in_specs, out_specs=out_specs, check_vma=False
        )

    def step(packet, *others):
        _, _, points, vibration, channels = packet.shape
        whole_blocks = channels == mesh.shape["rad"] * TILE
        whole_rows = points == mesh.shape["rad"] * TILE and vibration == sum(CHUNKS)
        if not (whole_blocks and whole_rows):
            return sharded(body_any)(packet, *others)

        return sharded(body_blocks)(packet, *others)

    return step
```

profile of v0, /device:TPU:0, one launch (start us, length us, event | category | flops | bytes accessed | tf_op | source)
XLA Modules:
  0.0 948.6 jit_solution(3922093955972818858)
XLA Ops:
  13.9 11.5 %pack.2 = (f32[8,2,1,2,128,128]{5,4,3,2,1,0:T(8,128)}, f32[8,2,2,2,128,128]{5,4,3,2,1,0:T(8,128)}, f32[8,2,2,2,128,128]{5,4,3,2,1,0:T(8,128)}, f32[8,2,1,2,128,128]{5,4,3,2,1,0:T(8,128)}) custom-call(f32[2,2,128,8,1024]{4,3,2,1,0:T(8,128)} %packet_ref.3), custom_call_target="tpu_custom_call" | custom-call | bytes 29360128 | tf_op jit(solution)/shard_map/pack/pallas_call | solution.py:290
  25.5 37.7 %all-to-all-done.refs_1_ = f32[8,2,2,2,128,128]{5,4,3,2,1,0:T(8,128)} async-done(((f32[8,2,2,2,128,128]{5,4,3,2,1,0:T(8,128)}), f32[8,2,2,2,128,128]{5,4,3,2,1,0:T(8,128)}, u32[]{:S(2)}, u32[]{:S(2)}) %all-to-all-start) | async-done | bytes 4194336 | tf_op jit(solution)/shard_map/all_to_all | solution.py:539
  66.7 17.2 %circulant.1 = (bf16[4,2,256,1024]{3,2,1,0:T(8,128)(2,1)}, bf16[4,2,256,1024]{3,2,1,0:T(8,128)(2,1)}) custom-call(f32[1,1024]{1,0:T(1,128)} %constant.34.real_ref, f32[1,1024]{1,0:T(1,128)} %constant.35.imag_ref), custom_call_target="tpu_custom_call" | custom-call | tf_op jit(solution)/shard_map/circulant/pallas_call | solution.py:209
  83.9 20.1 %kinetic.6.refs_0_ = f32[8,2,2,2,128,128]{5,4,3,2,1,0:T(8,128)} custom-call(f32[8,2,1,2,128,128]{5,4,3,2,1,0:T(8,128)} %gate.11.refs_0_, f32[8,2,2,2,128,128]{5,4,3,2,1,0:T(8,128)} %all-to-all-done.refs_1_, bf16[4,2,256,1024]{3,2,1,0:T(8,128)(2,1)} %get-tuple-element.44.refs_2_, bf16[4,2,256,1024]{3,2,1,0:T(8,128)(2,1)} %get-tuple-element.45.refs_3_), custom_call_target="tpu_custom_call" | custom-call | flops 12884901888 | bytes 16777216 | tf_op jit(solution)/shard_map/kinetic/pallas_call | solution.py:251
  110.0 12.4 %kinetic.7.refs_0_ = f32[8,2,1,2,128,128]{5,4,3,2,1,0:T(8,128)} custom-call(f32[8,2,2,2,128,128]{5,4,3,2,1,0:T(8,128)} %gate.12.refs_0_, f32[8,2,1,2,128,128]{5,4,3,2,1,0:T(8,128)} %copy-done.6, bf16[4,2,256,1024]{3,2,1,0:T(8,128)(2,1)} %get-tuple-element.44.refs_2_, bf16[4,2,256,1024]{3,2,1,0:T(8,128)(2,1)} %get-tuple-element.45.refs_3_), custom_call_target="tpu_custom_call" | custom-call | flops 6442450944 | bytes 12582912 | tf_op jit(solution)/shard_map/kinetic/pallas_call | solution.py:251
  122.4 36.7 %all-to-all-done.2.refs_1_.refs_2_.refs_3_.refs_9_.refs_10_ = f32[8,2,2,2,128,128]{5,4,3,2,1,0:T(8,128)} async-done(((f32[8,2,2,2,128,128]{5,4,3,2,1,0:T(8,128)}), f32[8,2,2,2,128,128]{5,4,3,2,1,0:T(8,128)}, u32[]{:S(2)}, u32[]{:S(2)}) %all-to-all-start.2) | async-done | bytes 4194336 | tf_op jit(solution)/shard_map/all_to_all | solution.py:539
  167.4 21.9 %all-to-all-done.3.refs_1_.refs_2_.refs_10_.refs_11_ = f32[8,2,1,2,128,128]{5,4,3,2,1,0:T(8,128)S(1)} async-done(((f32[8,2,1,2,128,128]{5,4,3,2,1,0:T(8,128)}), f32[8,2,1,2,128,128]{5,4,3,2,1,0:T(8,128)S(1)}, u32[]{:S(2)}, u32[]{:S(2)}) %all-to-all-start.3) | async-done | bytes 2097184 | tf_op jit(solution)/shard_map/all_to_all | solution.py:539
  209.9 35.3 %collective-permute-done.2.refs_4_ = f32[8,2,2,128,128]{4,3,2,1,0:T(8,128)} collective-permute-done((f32[8,2,2,128,128]{4,3,2,1,0:T(8,128)}, f32[8,2,2,128,128]{4,3,2,1,0:T(8,128)}, u32[]{:S(2)}, u32[]{:S(2)}) %collective-permute-start.2) | collective-permute-done | bytes 2097184 | tf_op jit(solution)/shard_map/ppermute | solution.py:544
  252.2 12.2 %shard_map.73 = (f32[8,2,2,128,128]{4,3,2,1,0:T(8,128)}, f32[8,2,2,128,128]{4,3,2,1,0:T(8,128)}) custom-call(s32[24,3]{1,0:T(8,128)} %copy.33.list_ref, f32[8,1,2,128,128]{4,3,2,1,0:T(8,128)} %get-tuple-element.84.refs_0_, f32[8,1,2,128,128]{4,3,2,1,0:T(8,128)} %get-tuple-element.85.refs_1_, ...), custom_call_target="tpu_custom_call" | custom-call | flops 3221225472 | bytes 16777216 | tf_op jit(solution)/shard_map/pallas_call | solution.py:480
  264.4 20.1 %kinetic.8.refs_0_ = f32[8,2,2,2,128,128]{5,4,3,2,1,0:T(8,128)} custom-call(f32[8,2,2,128,128]{4,3,2,1,0:T(8,128)} %get-tuple-element.46.refs_0_.refs_1_, f32[8,2,2,2,128,128]{5,4,3,2,1,0:T(8,128)} %all-to-all-done.4.refs_1_, bf16[4,2,256,1024]{3,2,1,0:T(8,128)(2,1)} %get-tuple-element.44.refs_2_, bf16[4,2,256,1024]{3,2,1,0:T(8,128)(2,1)} %get-tuple-element.45.refs_3_), custom_call_target="tpu_custom_call" | custom-call | flops 12884901888 | bytes 16777216 | tf_op jit(solution)/shard_map/kinetic/pallas_call | solution.py:251
  299.7 59.7 %collective-permute-done.4 = f32[8,1,2,128,128]{4,3,2,0,1:T(8,128)S(1)} collective-permute-done((f32[8,1,2,128,128]{4,3,2,0,1:T(8,128)}, f32[8,1,2,128,128]{4,3,2,0,1:T(8,128)S(1)}, u32[]{:S(2)}, u32[]{:S(2)}) %collective-permute-start.4) | collective-permute-done | bytes 1048608 | tf_op jit(solution)/shard_map/ppermute | solution.py:544
  373.9 14.2 %shard_map.75 = (f32[8,2,2,128,128]{4,3,2,1,0:T(8,128)}, f32[8,2,2,128,128]{4,3,2,1,0:T(8,128)}, f32[8,2,2,128,128]{4,3,2,1,0:T(8,128)}, f32[8,2,2,128,128]{4,3,2,1,0:T(8,128)}) custom-call(s32[24,3]{1,0:T(8,128)} %copy.33.list_ref, f32[8,1,2,128,128]{4,3,2,1,0:T(8,128)} %get-tuple-element.48.refs_0_.refs_2_, ...), custom_call_target="tpu_custom_call" | custom-call | flops 3221225472 | bytes 16777216 | tf_op jit(solution)/shard_map/pallas_call | solution.py:480
  402.6 15.9 %collective-permute-done.8.refs_4_ = f32[8,1,2,128,128]{4,3,2,1,0:T(8,128)S(1)} collective-permute-done((f32[8,1,2,128,128]{4,3,2,1,0:T(8,128)}, f32[8,1,2,128,128]{4,3,2,1,0:T(8,128)S(1)}, u32[]{:S(2)}, u32[]{:S(2)}) %collective-permute-start.8) | collective-permute-done | bytes 1048608 | tf_op jit(solution)/shard_map/ppermute | solution.py:544
  445.9 20.1 %kinetic.9.refs_0_ = f32[8,2,2,2,128,128]{5,4,3,2,1,0:T(8,128)} custom-call(f32[8,2,1,2,128,128]{5,4,3,2,1,0:T(8,128)} %gate.17.refs_0_, f32[8,2,2,2,128,128]{5,4,3,2,1,0:T(8,128)} %all-to-all-done.6.refs_1_, bf16[4,2,256,1024]{3,2,1,0:T(8,128)(2,1)} %get-tuple-element.44.refs_2_, bf16[4,2,256,1024]{3,2,1,0:T(8,128)(2,1)} %get-tuple-element.45.refs_3_), custom_call_target="tpu_custom_call" | custom-call | flops 12884901888 | bytes 16777216 | tf_op jit(solution)/shard_map/kinetic/pallas_call | solution.py:251
  490.0 36.9 %collective-permute-done.10.refs_3_ = f32[8,2,2,128,128]{4,3,2,1,0:T(8,128)} collective-permute-done((f32[8,2,2,128,128]{4,3,2,1,0:T(8,128)}, f32[8,2,2,128,128]{4,3,2,1,0:T(8,128)}, u32[]{:S(2)}, u32[]{:S(2)}) %collective-permute-start.10) | collective-permute-done | bytes 2097184 | tf_op jit(solution)/shard_map/ppermute | solution.py:544
  532.4 12.2 %shard_map.77 = (f32[8,2,2,128,128]{4,3,2,1,0:T(8,128)}, f32[8,2,2,128,128]{4,3,2,1,0:T(8,128)}) custom-call(s32[24,3]{1,0:T(8,128)} %copy.33.list_ref, f32[8,2,2,2,128,128]{5,4,3,2,1,0:T(8,128)} %gate.18.refs_0_, f32[8,2,2,2,128,128]{5,4,3,2,1,0:T(8,128)} %all-to-all-done.5.refs_1_.refs_2_.refs_10_.refs_11_, ...), custom_call_target="tpu_custom_call" | custom-call | flops 3221225472 | bytes 16777216 | tf_op jit(solution)/shard_map/pallas_call | solution.py:480
  563.5 12.4 %kinetic.10.refs_0_ = f32[8,2,1,2,128,128]{5,4,3,2,1,0:T(8,128)} custom-call(f32[2,8,1,2,128,128]{5,4,3,2,1,0:T(8,128)} %shard_map.78.refs_0_.refs_1_, f32[8,2,1,2,128,128]{5,4,3,2,1,0:T(8,128)} %copy-done.4, bf16[4,2,256,1024]{3,2,1,0:T(8,128)(2,1)} %get-tuple-element.44.refs_2_, bf16[4,2,256,1024]{3,2,1,0:T(8,128)(2,1)} %get-tuple-element.45.refs_3_), custom_call_target="tpu_custom_call" | custom-call | flops 6442450944 | bytes 12582912 | tf_op jit(solution)/shard_map/kinetic/pallas_call | solution.py:251
  595.4 25.9 %collective-permute-done.1 = f32[8,1,2,128,128]{4,3,2,0,1:T(8,128)S(1)} collective-permute-done((f32[8,1,2,128,128]{4,3,2,0,1:T(8,128)S(1)}, f32[8,1,2,128,128]{4,3,2,0,1:T(8,128)S(1)}, u32[]{:S(2)}, u32[]{:S(2)}) %collective-permute-start.1) | collective-permute-done | bytes 1048608 | tf_op jit(solution)/shard_map/ppermute | solution.py:545
  629.9 14.2 %shard_map.79 = (f32[8,2,2,128,128]{4,3,2,1,0:T(8,128)}, f32[8,2,2,128,128]{4,3,2,1,0:T(8,128)}, f32[8,2,2,128,128]{4,3,2,1,0:T(8,128)}, f32[8,2,2,128,128]{4,3,2,1,0:T(8,128)}) custom-call(s32[24,3]{1,0:T(8,128)} %copy.33.list_ref, f32[8,2,2,128,128]{4,3,2,1,0:T(8,128)} %get-tuple-element.78.refs_0_, f32[8,2,2,128,128]{4,3,2,1,0:T(8,128)} %get-tuple-element.77.refs_1_, ...), custom_call_target="tpu_custom_call" | custom-call | flops 3221225472 | bytes 16777216 | tf_op jit(solution)/shard_map/pallas_call | solution.py:480
  651.9 9.9 %collective-permute-done.16.refs_3_ = f32[8,2,2,128,128]{4,3,2,1,0:T(8,128)} collective-permute-done((f32[8,2,2,128,128]{4,3,2,1,0:T(8,128)}, f32[8,2,2,128,128]{4,3,2,1,0:T(8,128)}, u32[]{:S(2)}, u32[]{:S(2)}) %collective-permute-start.16) | collective-permute-done | bytes 2097184 | tf_op jit(solution)/shard_map/ppermute | solution.py:544
  672.0 12.2 %shard_map.80 = (f32[8,2,2,128,128]{4,3,2,1,0:T(8,128)}, f32[8,2,2,128,128]{4,3,2,1,0:T(8,128)}) custom-call(s32[24,3]{1,0:T(8,128)} %copy.33.list_ref, f32[8,2,1,2,128,128]{5,4,3,2,1,0:T(8,128)} %gate.20.refs_0_, f32[8,2,2,2,128,128]{5,4,3,2,1,0:T(8,128)} %all-to-all-done.8.refs_1_.refs_2_.refs_9_.refs_10_, ...), custom_call_target="tpu_custom_call" | custom-call | flops 3221225472 | bytes 16777216 | tf_op jit(solution)/shard_map/pallas_call | solution.py:480
  687.0 19.7 %collective-permute-done.18.refs_3_ = f32[8,2,2,128,128]{4,3,2,1,0:T(8,128)} collective-permute-done((f32[8,2,2,128,128]{4,3,2,1,0:T(8,128)}, f32[8,2,2,128,128]{4,3,2,1,0:T(8,128)}, u32[]{:S(2)}, u32[]{:S(2)}) %collective-permute-start.18) | collective-permute-done | bytes 2097184 | tf_op jit(solution)/shard_map/ppermute | solution.py:544
  709.3 12.4 %kinetic.11.refs_0_ = f32[8,2,1,2,128,128]{5,4,3,2,1,0:T(8,128)} custom-call(f32[8,2,2,128,128]{4,3,2,1,0:T(8,128)} %get-tuple-element.59.refs_0_.refs_1_, f32[8,2,1,2,128,128]{5,4,3,2,1,0:T(8,128)} %copy-done.5, bf16[4,2,256,1024]{3,2,1,0:T(8,128)(2,1)} %get-tuple-element.44.refs_2_, bf16[4,2,256,1024]{3,2,1,0:T(8,128)(2,1)} %get-tuple-element.45.refs_3_), custom_call_target="tpu_custom_call" | custom-call | flops 6442450944 | bytes 12582912 | tf_op jit(solution)/shard_map/kinetic/pallas_call | solution.py:251
  725.8 13.1 %shard_map.81.refs_0_ = f32[2,8,2,2,128,128]{5,4,3,2,1,0:T(8,128)} custom-call(s32[24,3]{1,0:T(8,128)} %copy.33.list_ref, f32[8,2,1,2,128,128]{5,4,3,2,1,0:T(8,128)} %gate.21.refs_0_, f32[8,2,2,128,128]{4,3,2,1,0:T(8,128)} %get-tuple-element.50.refs_2_.refs_1_, f32[8,2,2,128,128]{4,3,2,1,0:T(8,128)} %get-tuple-element.60.refs_2_, ...), custom_call_target="tpu_custom_call" | custom-call | flops 3221225472 | bytes 16777216 | tf_op jit(solution)/shard_map/pallas_call | solution.py:480
  738.8 12.8 %collective-permute-done.20.refs_3_ = f32[8,2,2,128,128]{4,3,2,1,0:T(8,128)} collective-permute-done((f32[8,2,2,128,128]{4,3,2,1,0:T(8,128)}, f32[8,2,2,128,128]{4,3,2,1,0:T(8,128)}, u32[]{:S(2)}, u32[]{:S(2)}) %collective-permute-start.20) | collective-permute-done | bytes 2097184 | tf_op jit(solution)/shard_map/ppermute | solution.py:544
  751.6 10.2 %collective-permute-done.21.refs_4_ = f32[8,2,2,128,128]{4,3,2,1,0:T(8,128)} collective-permute-done((f32[8,2,2,128,128]{4,3,2,1,0:T(8,128)}, f32[8,2,2,128,128]{4,3,2,1,0:T(8,128)}, u32[]{:S(2)}, u32[]{:S(2)}) %collective-permute-start.21) | collective-permute-done | bytes 2097184 | tf_op jit(solution)/shard_map/ppermute | solution.py:545
  761.9 13.1 %shard_map.82.refs_0_.refs_2_ = f32[2,8,2,2,128,128]{5,4,3,2,1,0:T(8,128)} custom-call(s32[24,3]{1,0:T(8,128)} %copy.33.list_ref, f32[2,8,2,2,128,128]{5,4,3,2,1,0:T(8,128)} %shard_map.81.refs_0_, f32[8,2,2,128,128]{4,3,2,1,0:T(8,128)} %get-tuple-element.58.refs_2_.refs_1_, f32[8,2,2,128,128]{4,3,2,1,0:T(8,128)} %get-tuple-element.63.refs_2_, ...), custom_call_target="tpu_custom_call" | custom-call | flops 3221225472 | bytes 16777216 | tf_op jit(solution)/shard_map/pallas_call | solution.py:480
  784.6 11.3 %collective-permute-done.22.refs_3_ = f32[8,2,2,128,128]{4,3,2,1,0:T(8,128)} collective-permute-done((f32[8,2,2,128,128]{4,3,2,1,0:T(8,128)}, f32[8,2,2,128,128]{4,3,2,1,0:T(8,128)}, u32[]{:S(2)}, u32[]{:S(2)}) %collective-permute-start.22) | collective-permute-done | bytes 2097184 | tf_op jit(solution)/shard_map/ppermute | solution.py:544
  805.1 14.2 %shard_map.84 = (f32[8,2,2,128,128]{4,3,2,1,0:T(8,128)}, f32[8,2,2,128,128]{4,3,2,1,0:T(8,128)}, f32[8,2,2,128,128]{4,3,2,1,0:T(8,128)}, f32[8,2,2,128,128]{4,3,2,1,0:T(8,128)}) custom-call(s32[24,3]{1,0:T(8,128)} %copy.33.list_ref, f32[8,1,2,128,128]{4,3,2,1,0:T(8,128)} %get-tuple-element.66.refs_0_.refs_1_, ...), custom_call_target="tpu_custom_call" | custom-call | flops 3221225472 | bytes 16777216 | tf_op jit(solution)/shard_map/pallas_call | solution.py:480
  829.0 58.0 %collective-permute-done.24.refs_3_ = f32[8,1,2,128,128]{4,3,2,1,0:T(8,128)} collective-permute-done((f32[8,1,2,128,128]{4,3,2,1,0:T(8,128)}, f32[8,1,2,128,128]{4,3,2,1,0:T(8,128)}, u32[]{:S(2)}, u32[]{:S(2)}) %collective-permute-start.24) | collective-permute-done | bytes 1048608 | tf_op jit(solution)/shard_map/ppermute | solution.py:544
  905.4 13.0 %shard_map.86.refs_0_.refs_3_ = f32[2,8,2,2,128,128]{5,4,3,2,1,0:T(8,128)} custom-call(s32[24,3]{1,0:T(8,128)} %copy.33.list_ref, f32[8,1,2,128,128]{4,3,2,1,0:T(8,128)} %get-tuple-element.70.refs_0_.refs_1_, f32[8,2,2,128,128]{4,3,2,1,0:T(8,128)} %get-tuple-element.68.refs_0_.refs_1_, f32[8,2,2,128,128]{4,3,2,1,0:T(8,128)} %get-tuple-element.71.refs_2_, ...), custom_call_target="tpu_custom_call" | custom-call | flops 3221225472 | bytes 16777216 | tf_op jit(solution)/shard_map/pallas_call | solution.py:480
  936.1 12.4 %unpack.1 = f32[2,2,128,8,1024]{4,3,2,1,0:T(8,128)} custom-call(f32[2,8,2,2,128,128]{5,4,3,2,1,0:T(8,128)} %shard_map.81.refs_0_, f32[2,8,1,2,128,128]{5,4,3,2,1,0:T(8,128)} %shard_map.78.refs_0_.refs_1_, f32[2,8,2,2,128,128]{5,4,3,2,1,0:T(8,128)} %shard_map.82.refs_0_.refs_2_, f32[2,8,2,2,128,128]{5,4,3,2,1,0:T(8,128)} %shard_map.86.refs_0_.refs_3_, ...), custom_call_target="tpu_custom_call" | custom-call | tf_op jit(solution)/shard_map/unpack/pallas_call | solution.py:325
  (149 shorter events, 299.4 us)
Async XLA Ops:
  8.7 54.4 %all-to-all-start = ((f32[8,2,2,2,128,128]{5,4,3,2,1,0:T(8,128)}), f32[8,2,2,2,128,128]{5,4,3,2,1,0:T(8,128)}, u32[]{:S(2)}, u32[]{:S(2)}) async-start(f32[8,2,2,2,128,128]{5,4,3,2,1,0:T(8,128)} %pack.3), calls=%async_computation | async-start | bytes 8388608 | tf_op jit(solution)/shard_map/all_to_all | solution.py:539
  105.4 53.7 %all-to-all-start.2 = ((f32[8,2,2,2,128,128]{5,4,3,2,1,0:T(8,128)}), f32[8,2,2,2,128,128]{5,4,3,2,1,0:T(8,128)}, u32[]{:S(2)}, u32[]{:S(2)}) async-start(f32[8,2,2,2,128,128]{5,4,3,2,1,0:T(8,128)} %gate.12.refs_0_), calls=%async_computation.2 | async-start | bytes 8388608 | tf_op jit(solution)/shard_map/all_to_all | solution.py:539
  190.6 73.8 %all-to-all-start.4 = ((f32[8,2,2,2,128,128]{5,4,3,2,1,0:T(8,128)}), f32[8,2,2,2,128,128]{5,4,3,2,1,0:T(8,128)}, u32[]{:S(2)}, u32[]{:S(2)}) async-start(f32[8,2,2,2,128,128]{5,4,3,2,1,0:T(8,128)} %gate.14), calls=%async_computation.4 | async-start | bytes 8388608 | tf_op jit(solution)/shard_map/all_to_all | solution.py:539
  195.2 49.9 %collective-permute-start.2 = (f32[8,2,2,128,128]{4,3,2,1,0:T(8,128)}, f32[8,2,2,128,128]{4,3,2,1,0:T(8,128)}, u32[]{:S(2)}, u32[]{:S(2)}) collective-permute-start(f32[8,2,2,128,128]{4,3,2,1,0:T(8,128)} %get-tuple-element.82.refs_3_), channel_id=1, source_target_pairs={{0,8},{8,16},{16,24},{1,9},{9,17},{17,25},{2,10},{10,18},{18,26},{... | collective-permute-start | bytes 6291464 | tf_op jit(solution)/shard_map/ppermute | solution.py:544
  200.9 49.6 %collective-permute-start.3 = (f32[8,2,2,128,128]{4,3,2,1,0:T(8,128)S(1)}, f32[8,2,2,128,128]{4,3,2,1,0:T(8,128)}, u32[]{:S(2)}, u32[]{:S(2)}) collective-permute-start(f32[8,2,2,128,128]{4,3,2,1,0:T(8,128)S(1)} %copy-done.8), channel_id=1, source_target_pairs={{8,0},{16,8},{24,16},{9,1},{17,9},{25,17},{10,2},{18,10},{26,18},{... | collective-permute-start | bytes 6291464 | tf_op jit(solution)/shard_map/ppermute | solution.py:545
  284.4 103.6 %all-to-all-start.5 = ((f32[8,2,2,2,128,128]{5,4,3,2,1,0:T(8,128)}), f32[8,2,2,2,128,128]{5,4,3,2,1,0:T(8,128)}, u32[]{:S(2)}, u32[]{:S(2)}) async-start(f32[8,2,2,2,128,128]{5,4,3,2,1,0:T(8,128)} %gate.15.refs_0_), calls=%async_computation.5 | async-start | bytes 8388608 | tf_op jit(solution)/shard_map/all_to_all | solution.py:539
  289.1 84.7 %collective-permute-start.6 = (f32[8,2,2,128,128]{4,3,2,1,0:T(8,128)}, f32[8,2,2,128,128]{4,3,2,1,0:T(8,128)}, u32[]{:S(2)}, u32[]{:S(2)}) collective-permute-start(f32[8,2,2,128,128]{4,3,2,1,0:T(8,128)} %get-tuple-element.49.refs_2_), channel_id=1, source_target_pairs={{0,8},{8,16},{16,24},{1,9},{9,17},{17,25},{2,10},{10,18},{18,26},{... | collective-permute-start | bytes 6291464 | tf_op jit(solution)/shard_map/ppermute | solution.py:544
  292.5 81.3 %collective-permute-start.7 = (f32[8,2,2,128,128]{4,3,2,1,0:T(8,128)S(1)}, f32[8,2,2,128,128]{4,3,2,1,0:T(8,128)}, u32[]{:S(2)}, u32[]{:S(2)}) collective-permute-start(f32[8,2,2,128,128]{4,3,2,1,0:T(8,128)S(1)} %copy-done.13), channel_id=1, source_target_pairs={{8,0},{16,8},{24,16},{9,1},{17,9},{25,17},{10,2},{18,10},{26,18},{... | collective-permute-start | bytes 6291464 | tf_op jit(solution)/shard_map/ppermute | solution.py:545
  293.8 65.6 %collective-permute-start.4 = (f32[8,1,2,128,128]{4,3,2,0,1:T(8,128)}, f32[8,1,2,128,128]{4,3,2,0,1:T(8,128)S(1)}, u32[]{:S(2)}, u32[]{:S(2)}) collective-permute-start(f32[8,1,2,128,128]{4,3,2,0,1:T(8,128)} %get-tuple-element.86), channel_id=1, source_target_pairs={{0,8},{8,16},{16,24},{1,9},{9,17},{17,25},{2,10},{10,18},{18,26},{... | collective-permute-start | bytes 3145736 | tf_op jit(solution)/shard_map/ppermute | solution.py:544
  298.4 66.1 %collective-permute-start.5 = (f32[8,1,2,128,128]{4,3,2,0,1:T(8,128)S(1)}, f32[8,1,2,128,128]{4,3,2,0,1:T(8,128)S(1)}, u32[]{:S(2)}, u32[]{:S(2)}) collective-permute-start(f32[8,1,2,128,128]{4,3,2,0,1:T(8,128)S(1)} %get-tuple-element.83), channel_id=1, source_target_pairs={{8,0},{16,8},{24,16},{9,1},{17,9},{25,17},{10,2},{18,10},{26,18},{... | collective-permute-start | bytes 3145736 | tf_op jit(solution)/shard_map/ppermute | solution.py:545
  388.1 54.0 %all-to-all-start.6 = ((f32[8,2,2,2,128,128]{5,4,3,2,1,0:T(8,128)}), f32[8,2,2,2,128,128]{5,4,3,2,1,0:T(8,128)}, u32[]{:S(2)}, u32[]{:S(2)}) async-start(f32[8,2,2,2,128,128]{5,4,3,2,1,0:T(8,128)} %gate.16), calls=%async_computation.6 | async-start | bytes 8388608 | tf_op jit(solution)/shard_map/all_to_all | solution.py:539
  473.5 102.4 %all-to-all-start.8 = ((f32[8,2,2,2,128,128]{5,4,3,2,1,0:T(8,128)}), f32[8,2,2,2,128,128]{5,4,3,2,1,0:T(8,128)}, u32[]{:S(2)}, u32[]{:S(2)}) async-start(f32[8,2,2,2,128,128]{5,4,3,2,1,0:T(8,128)} %gate.18.refs_0_), calls=%async_computation.8 | async-start | bytes 8388608 | tf_op jit(solution)/shard_map/all_to_all | solution.py:539
  481.9 50.5 %collective-permute-start.11 = (f32[8,2,2,128,128]{4,3,2,1,0:T(8,128)S(1)}, f32[8,2,2,128,128]{4,3,2,1,0:T(8,128)}, u32[]{:S(2)}, u32[]{:S(2)}) collective-permute-start(f32[8,2,2,128,128]{4,3,2,1,0:T(8,128)S(1)} %copy-done.9), channel_id=1, source_target_pairs={{8,0},{16,8},{24,16},{9,1},{17,9},{25,17},{10,2},{18,10},{26,18},{... | collective-permute-start | bytes 6291464 | tf_op jit(solution)/shard_map/ppermute | solution.py:545
  483.2 66.2 %collective-permute-start.12 = (f32[8,1,2,128,128]{4,3,2,1,0:T(8,128)}, f32[8,1,2,128,128]{4,3,2,1,0:T(8,128)}, u32[]{:S(2)}, u32[]{:S(2)}) collective-permute-start(f32[8,1,2,128,128]{4,3,2,1,0:T(8,128)} %get-tuple-element.54.refs_2_), channel_id=1, source_target_pairs={{0,8},{8,16},{16,24},{1,9},{9,17},{17,25},{2,10},{10,18},{18,26},{... | collective-permute-start | bytes 3145736 | tf_op jit(solution)/shard_map/ppermute | solution.py:544
  488.8 66.1 %collective-permute-start.13 = (f32[8,1,2,128,128]{4,3,2,1,0:T(8,128)S(1)}, f32[8,1,2,128,128]{4,3,2,1,0:T(8,128)}, u32[]{:S(2)}, u32[]{:S(2)}) collective-permute-start(f32[8,1,2,128,128]{4,3,2,1,0:T(8,128)S(1)} %copy-done.11), channel_id=1, source_target_pairs={{8,0},{16,8},{24,16},{9,1},{17,9},{25,17},{10,2},{18,10},{26,18},{... | collective-permute-start | bytes 3145736 | tf_op jit(solution)/shard_map/ppermute | solution.py:545
  544.6 85.3 %collective-permute-start.14 = (f32[8,2,2,128,128]{4,3,2,1,0:T(8,128)}, f32[8,2,2,128,128]{4,3,2,1,0:T(8,128)}, u32[]{:S(2)}, u32[]{:S(2)}) collective-permute-start(f32[8,2,2,128,128]{4,3,2,1,0:T(8,128)} %get-tuple-element.57.refs_3_), channel_id=1, source_target_pairs={{0,8},{8,16},{16,24},{1,9},{9,17},{17,25},{2,10},{10,18},{18,26},{... | collective-permute-start | bytes 6291464 | tf_op jit(solution)/shard_map/ppermute | solution.py:544
  547.2 82.6 %collective-permute-start.15 = (f32[8,2,2,128,128]{4,3,2,1,0:T(8,128)}, f32[8,2,2,128,128]{4,3,2,1,0:T(8,128)}, u32[]{:S(2)}, u32[]{:S(2)}) collective-permute-start(f32[8,2,2,128,128]{4,3,2,1,0:T(8,128)} %get-tuple-element.53.refs_0_.refs_2_), channel_id=1, source_target_pairs={{8,0},{16,8},{24,16},{9,1},{17,9},{25,17},{10,2},{18,10},{26,18},{... | collective-permute-start | bytes 6291464 | tf_op jit(solution)/shard_map/ppermute | solution.py:545
  575.9 68.2 %all-to-all-start.9 = ((f32[8,2,1,2,128,128]{5,4,3,2,1,0:T(8,128)}), f32[8,2,1,2,128,128]{5,4,3,2,1,0:T(8,128)S(1)}, u32[]{:S(2)}, u32[]{:S(2)}) async-start(f32[8,2,1,2,128,128]{5,4,3,2,1,0:T(8,128)} %gate.19), calls=%async_computation.9 | async-start | bytes 4194304 | tf_op jit(solution)/shard_map/all_to_all | solution.py:539
  592.3 69.5 %collective-permute-start.16 = (f32[8,2,2,128,128]{4,3,2,1,0:T(8,128)}, f32[8,2,2,128,128]{4,3,2,1,0:T(8,128)}, u32[]{:S(2)}, u32[]{:S(2)}) collective-permute-start(f32[8,2,2,128,128]{4,3,2,1,0:T(8,128)} %get-tuple-element.77.refs_1_), channel_id=1, source_target_pairs={{0,8},{8,16},{16,24},{1,9},{9,17},{17,25},{2,10},{10,18},{18,26},{... | collective-permute-start | bytes 6291464 | tf_op jit(solution)/shard_map/ppermute | solution.py:544
  621.3 50.7 %collective-permute-start.17 = (f32[8,2,2,128,128]{4,3,2,1,0:T(8,128)}, f32[8,2,2,128,128]{4,3,2,1,0:T(8,128)}, u32[]{:S(2)}, u32[]{:S(2)}) collective-permute-start(f32[8,2,2,128,128]{4,3,2,1,0:T(8,128)} %get-tuple-element.78.refs_0_), channel_id=1, source_target_pairs={{8,0},{16,8},{24,16},{9,1},{17,9},{25,17},{10,2},{18,10},{26,18},{... | collective-permute-start | bytes 6291464 | tf_op jit(solution)/shard_map/ppermute | solution.py:545
  624.1 82.6 %collective-permute-start.18 = (f32[8,2,2,128,128]{4,3,2,1,0:T(8,128)}, f32[8,2,2,128,128]{4,3,2,1,0:T(8,128)}, u32[]{:S(2)}, u32[]{:S(2)}) collective-permute-start(f32[8,2,2,128,128]{4,3,2,1,0:T(8,128)} %get-tuple-element.60.refs_2_), channel_id=1, source_target_pairs={{0,8},{8,16},{16,24},{1,9},{9,17},{17,25},{2,10},{10,18},{18,26},{... | collective-permute-start | bytes 6291464 | tf_op jit(solution)/shard_map/ppermute | solution.py:544
  645.4 62.5 %all-to-all-start.10 = ((f32[8,2,1,2,128,128]{5,4,3,2,1,0:T(8,128)}), f32[8,2,1,2,128,128]{5,4,3,2,1,0:T(8,128)S(1)}, u32[]{:S(2)}, u32[]{:S(2)}) async-start(f32[8,2,1,2,128,128]{5,4,3,2,1,0:T(8,128)} %gate.20.refs_0_), calls=%async_computation.10 | async-start | bytes 4194304 | tf_op jit(solution)/shard_map/all_to_all | solution.py:539
  649.3 76.5 %collective-permute-start.19 = (f32[8,2,2,128,128]{4,3,2,1,0:T(8,128)}, f32[8,2,2,128,128]{4,3,2,1,0:T(8,128)}, u32[]{:S(2)}, u32[]{:S(2)}) collective-permute-start(f32[8,2,2,128,128]{4,3,2,1,0:T(8,128)} %get-tuple-element.50.refs_2_.refs_1_), channel_id=1, source_target_pairs={{8,0},{16,8},{24,16},{9,1},{17,9},{25,17},{10,2},{18,10},{26,18},{... | collective-permute-start | bytes 6291464 | tf_op jit(solution)/shard_map/ppermute | solution.py:545
  650.6 111.3 %collective-permute-start.21 = (f32[8,2,2,128,128]{4,3,2,1,0:T(8,128)}, f32[8,2,2,128,128]{4,3,2,1,0:T(8,128)}, u32[]{:S(2)}, u32[]{:S(2)}) collective-permute-start(f32[8,2,2,128,128]{4,3,2,1,0:T(8,128)} %get-tuple-element.58.refs_2_.refs_1_), channel_id=1, source_target_pairs={{8,0},{16,8},{24,16},{9,1},{17,9},{25,17},{10,2},{18,10},{26,18},{... | collective-permute-start | bytes 6291464 | tf_op jit(solution)/shard_map/ppermute | solution.py:545
  661.7 89.9 %collective-permute-start.20 = (f32[8,2,2,128,128]{4,3,2,1,0:T(8,128)}, f32[8,2,2,128,128]{4,3,2,1,0:T(8,128)}, u32[]{:S(2)}, u32[]{:S(2)}) collective-permute-start(f32[8,2,2,128,128]{4,3,2,1,0:T(8,128)} %get-tuple-element.63.refs_2_), channel_id=1, source_target_pairs={{0,8},{8,16},{16,24},{1,9},{9,17},{17,25},{2,10},{10,18},{18,26},{... | collective-permute-start | bytes 6291464 | tf_op jit(solution)/shard_map/ppermute | solution.py:544
  684.2 111.8 %collective-permute-start.22 = (f32[8,2,2,128,128]{4,3,2,1,0:T(8,128)}, f32[8,2,2,128,128]{4,3,2,1,0:T(8,128)}, u32[]{:S(2)}, u32[]{:S(2)}) collective-permute-start(f32[8,2,2,128,128]{4,3,2,1,0:T(8,128)} %get-tuple-element.67.refs_2_), channel_id=1, source_target_pairs={{0,8},{8,16},{16,24},{1,9},{9,17},{17,25},{2,10},{10,18},{18,26},{... | collective-permute-start | bytes 6291464 | tf_op jit(solution)/shard_map/ppermute | solution.py:544
  706.7 98.4 %collective-permute-start.23 = (f32[8,2,2,128,128]{4,3,2,1,0:T(8,128)}, f32[8,2,2,128,128]{4,3,2,1,0:T(8,128)}, u32[]{:S(2)}, u32[]{:S(2)}) collective-permute-start(f32[8,2,2,128,128]{4,3,2,1,0:T(8,128)} %get-tuple-element.59.refs_0_.refs_1_), channel_id=1, source_target_pairs={{8,0},{16,8},{24,16},{9,1},{17,9},{25,17},{10,2},{18,10},{26,18},{... | collective-permute-start | bytes 6291464 | tf_op jit(solution)/shard_map/ppermute | solution.py:545
  721.7 53.3 %all-to-all-start.11 = ((f32[8,2,1,2,128,128]{5,4,3,2,1,0:T(8,128)}), f32[8,2,1,2,128,128]{5,4,3,2,1,0:T(8,128)S(1)}, u32[]{:S(2)}, u32[]{:S(2)}) async-start(f32[8,2,1,2,128,128]{5,4,3,2,1,0:T(8,128)} %gate.21.refs_0_), calls=%async_computation.11 | async-start | bytes 4194304 | tf_op jit(solution)/shard_map/all_to_all | solution.py:539
  819.3 84.8 %collective-permute-start.26 = (f32[8,2,2,128,128]{4,3,2,1,0:T(8,128)}, f32[8,2,2,128,128]{4,3,2,1,0:T(8,128)S(1)}, u32[]{:S(2)}, u32[]{:S(2)}) collective-permute-start(f32[8,2,2,128,128]{4,3,2,1,0:T(8,128)} %get-tuple-element.71.refs_2_), channel_id=1, source_target_pairs={{0,8},{8,16},{16,24},{1,9},{9,17},{17,25},{2,10},{10,18},{18,26},{... | collective-permute-start | bytes 6291464 | tf_op jit(solution)/shard_map/ppermute | solution.py:544
  820.9 83.3 %collective-permute-start.27 = (f32[8,2,2,128,128]{4,3,2,1,0:T(8,128)}, f32[8,2,2,128,128]{4,3,2,1,0:T(8,128)}, u32[]{:S(2)}, u32[]{:S(2)}) collective-permute-start(f32[8,2,2,128,128]{4,3,2,1,0:T(8,128)} %get-tuple-element.68.refs_0_.refs_1_), channel_id=1, source_target_pairs={{8,0},{16,8},{24,16},{9,1},{17,9},{25,17},{10,2},{18,10},{26,18},{... | collective-permute-start | bytes 6291464 | tf_op jit(solution)/shard_map/ppermute | solution.py:545
  822.2 64.9 %collective-permute-start.24 = (f32[8,1,2,128,128]{4,3,2,1,0:T(8,128)}, f32[8,1,2,128,128]{4,3,2,1,0:T(8,128)}, u32[]{:S(2)}, u32[]{:S(2)}) collective-permute-start(f32[8,1,2,128,128]{4,3,2,1,0:T(8,128)} %get-tuple-element.69.refs_2_), channel_id=1, source_target_pairs={{0,8},{8,16},{16,24},{1,9},{9,17},{17,25},{2,10},{10,18},{18,26},{... | collective-permute-start | bytes 3145736 | tf_op jit(solution)/shard_map/ppermute | solution.py:544
  827.7 63.6 %collective-permute-start.25 = (f32[8,1,2,128,128]{4,3,2,1,0:T(8,128)S(1)}, f32[8,1,2,128,128]{4,3,2,1,0:T(8,128)}, u32[]{:S(2)}, u32[]{:S(2)}) collective-permute-start(f32[8,1,2,128,128]{4,3,2,1,0:T(8,128)S(1)} %copy-done.12), channel_id=1, source_target_pairs={{8,0},{16,8},{24,16},{9,1},{17,9},{25,17},{10,2},{18,10},{26,18},{... | collective-permute-start | bytes 3145736 | tf_op jit(solution)/shard_map/ppermute | solution.py:545
  (33 other events, 502.6 us)
where the time goes:
time: 952 us; the launch traced here: 949 us
  waiting for transfers between devices  461 us (48%)
  Pallas kernels  318 us (33%)
  starting transfers between devices  130 us (14%)
  local copies, waits for them, and re-layouts  33.9 us (4%)
    ppermute x15, waiting for transfers between devices, halo(): below = lax.ppermute(last, 'hel', forward)  265 us
    pallas_call x15, Pallas kernels, taylor(): pl.pallas_call(functools.partial(taylor_kernel, degree, helices, len(afte...  171 us
    all_to_all x12, waiting for transfers between devices, send(): previous = (exchange(value),)  112 us
    pallas_call x6, Pallas kernels, kinetic(): pl.pallas_call(kinetic_kernel, grid=(helices, count), in_specs=[*[ANYWHER...  97.4 us
    ppermute x15, waiting for transfers between devices, halo(): halos[c] = (below, lax.ppermute(first, 'hel', backward))  83.4 us
    ppermute x15, starting transfers between devices, halo(): below = lax.ppermute(last, 'hel', forward)  59.1 us
    all_to_all x12, starting transfers between devices, send(): previous = (exchange(value),)  51.8 us
    pallas_call x2, Pallas kernels, pack(): pl.pallas_call(functools.partial(pack_kernel, chunks), grid=(helices, par...  20.3 us
  transfers between devices with their start and end apart: 42, of which 27 were waited for; matrix products, arithmetic and copies ran while one was open for 3% of the time, Pallas kernels for 27%

commit v1 on v0

--- a/solution.py
+++ b/solution.py
@@ -15,7 +15,7 @@
 CHUNKS = (2, 1, 2, 2, 1)
 EARLY = (4,)
 PLAN = (
-    ("F", 0), ("F", 1), ("K", 0), ("B", 0), ("K", 1), ("B", 1), ("E", 0), ("F", 2), ("E", 1),
+    ("F", 0), ("F", 1), ("K", 0), ("B", 0), ("K", 1), ("E", 0), ("B", 1), ("F", 2), ("E", 1),
     ("T", 0), ("K", 2), ("B", 2), ("T", 1), ("T", 0), ("F", 3), ("E", 2), ("T", 1), ("F", 4),
     ("K", 3), ("B", 3), ("T", 2), ("T", 1), ("K", 4), ("B", 4), ("E", 3), ("T", 2), ("G", 4),
     ("T", 3), ("L", 4), ("C", 4), ("T", 0), ("T", 2), ("T", 4), ("T", 3), ("T", 4), ("T", 3),
@@ -528,12 +528,12 @@
     factor = jnp.broadcast_to(radial_factor_of(radial)[:, None], (radial, TILE))
 
     spectra, terms, halos, sums, degrees = {}, {}, {}, {}, {}
-    previous, latest = (), ()
+    previous = ()
 
     def send(value):
         nonlocal previous, latest
-        afters = [a for a in (*previous, *latest) if a is not value]
-        if afters:
+        if previous:
+            afters = [a for a in (*previous, *latest) if a is not value]
             value = gate(value, *afters)
             latest = (value,)
         previous = (exchange(value),)
@@ -544,8 +544,10 @@
         below = lax.ppermute(last, "hel", forward)
         halos[c] = below, lax.ppermute(first, "hel", backward)
 
+    latest = (high,)
     for c in EARLY:
-        halo(c, 0, packed[c][:, 0], packed[c][:, -1])
+        latest += packed[c][:, 0], packed[c][:, -1]
+        halo(c, 0, *latest[-2:])
 
     def run(kind, c):
         nonlocal latest

time: 952 us -> 945 us (level)
  waiting for transfers between devices: 461 us -> 426 us
  blocking collectives: 0 us -> 30.9 us
    all_to_all x12 -> x11, waiting for transfers between devices: 112 us -> 75.6 us  [send(): previous = (exchange(value),)]
    all_to_all x0 -> x1, blocking collectives: none -> 30.9 us  [send(): previous = (exchange(value),)]
    all_to_all x12 -> x11, starting transfers between devices: 51.8 us -> 48.2 us  [send(): previous = (exchange(value),)]
  transfers between devices with their start and end apart: 42 -> 41, of which waited for: 27 -> 27; matrix products, arithmetic and copies ran while one was open for 3% -> 2% of each run, Pallas kernels for 27% -> 27%
where the time goes in v1:
time: 945 us; the launch traced here: 942 us
  waiting for transfers between devices  426 us (45%)
  Pallas kernels  319 us (34%)
  starting transfers between devices  127 us (13%)
  local copies, waits for them, and re-layouts  33.4 us (4%)
  blocking collectives  30.9 us (3%)
    ppermute x15, waiting for transfers between devices, halo(): below = lax.ppermute(last, 'hel', forward)  265 us
    pallas_call x15, Pallas kernels, taylor(): pl.pallas_call(functools.partial(taylor_kernel, degree, helices, len(afte...  171 us
    pallas_call x6, Pallas kernels, kinetic(): pl.pallas_call(kinetic_kernel, grid=(helices, count), in_specs=[*[ANYWHER...  97.5 us
    ppermute x15, waiting for transfers between devices, halo(): halos[c] = (below, lax.ppermute(first, 'hel', backward))  85.4 us
    all_to_all x11, waiting for transfers between devices, send(): previous = (exchange(value),)  75.6 us
    ppermute x15, starting transfers between devices, halo(): below = lax.ppermute(last, 'hel', forward)  59.6 us
    all_to_all x11, starting transfers between devices, send(): previous = (exchange(value),)  48.2 us
    all_to_all x1, blocking collectives, send(): previous = (exchange(value),)  30.9 us
  transfers between devices with their start and end apart: 41, of which 27 were waited for; matrix products, arithmetic and copies ran while one was open for 2% of the time, Pallas kernels for 27%

profile of v1, /device:TPU:0, one launch (start us, length us, event | category | flops | bytes accessed | tf_op | source)
XLA Modules:
  0.0 942.0 jit_solution(3252303107424396592)
XLA Ops:
  13.9 11.6 %pack.2 = (f32[8,2,1,2,128,128]{5,4,3,2,1,0:T(8,128)}, f32[8,2,2,2,128,128]{5,4,3,2,1,0:T(8,128)}, f32[8,2,2,2,128,128]{5,4,3,2,1,0:T(8,128)}, f32[8,2,1,2,128,128]{5,4,3,2,1,0:T(8,128)}) custom-call(f32[2,2,128,8,1024]{4,3,2,1,0:T(8,128)} %packet_ref.3), custom_call_target="tpu_custom_call" | custom-call | bytes 29360128 | tf_op jit(solution)/shard_map/pack/pallas_call | solution.py:290
  25.4 17.2 %circulant.1 = (bf16[4,2,256,1024]{3,2,1,0:T(8,128)(2,1)}, bf16[4,2,256,1024]{3,2,1,0:T(8,128)(2,1)}) custom-call(f32[1,1024]{1,0:T(1,128)} %constant.34.real_ref, f32[1,1024]{1,0:T(1,128)} %constant.35.imag_ref), custom_call_target="tpu_custom_call" | custom-call | tf_op jit(solution)/shard_map/circulant/pallas_call | solution.py:209
  46.4 16.6 %all-to-all-done.refs_1_ = f32[8,2,2,2,128,128]{5,4,3,2,1,0:T(8,128)} async-done(((f32[8,2,2,2,128,128]{5,4,3,2,1,0:T(8,128)}), f32[8,2,2,2,128,128]{5,4,3,2,1,0:T(8,128)}, u32[]{:S(2)}, u32[]{:S(2)}) %all-to-all-start) | async-done | bytes 4194336 | tf_op jit(solution)/shard_map/all_to_all | solution.py:539
  66.7 20.1 %kinetic.6.refs_0_ = f32[8,2,2,2,128,128]{5,4,3,2,1,0:T(8,128)} custom-call(f32[8,2,1,2,128,128]{5,4,3,2,1,0:T(8,128)} %gate.11.refs_0_, f32[8,2,2,2,128,128]{5,4,3,2,1,0:T(8,128)} %all-to-all-done.refs_1_, bf16[4,2,256,1024]{3,2,1,0:T(8,128)(2,1)} %get-tuple-element.44.refs_2_, bf16[4,2,256,1024]{3,2,1,0:T(8,128)(2,1)} %get-tuple-element.45.refs_3_), custom_call_target="tpu_custom_call" | custom-call | flops 12884901888 | bytes 16777216 | tf_op jit(solution)/shard_map/kinetic/pallas_call | solution.py:251
  99.1 12.4 %kinetic.7.refs_0_ = f32[8,2,1,2,128,128]{5,4,3,2,1,0:T(8,128)} custom-call(f32[8,2,2,2,128,128]{5,4,3,2,1,0:T(8,128)} %gate.12.refs_0_, f32[8,2,1,2,128,128]{5,4,3,2,1,0:T(8,128)} %copy-done.5, bf16[4,2,256,1024]{3,2,1,0:T(8,128)(2,1)} %get-tuple-element.44.refs_2_, bf16[4,2,256,1024]{3,2,1,0:T(8,128)(2,1)} %get-tuple-element.45.refs_3_), custom_call_target="tpu_custom_call" | custom-call | flops 6442450944 | bytes 12582912 | tf_op jit(solution)/shard_map/kinetic/pallas_call | solution.py:251
  111.5 36.7 %all-to-all-done.2.refs_1_.refs_2_.refs_3_.refs_9_.refs_10_ = f32[8,2,2,2,128,128]{5,4,3,2,1,0:T(8,128)} async-done(((f32[8,2,2,2,128,128]{5,4,3,2,1,0:T(8,128)}), f32[8,2,2,2,128,128]{5,4,3,2,1,0:T(8,128)}, u32[]{:S(2)}, u32[]{:S(2)}) %all-to-all-start.2) | async-done | bytes 4194336 | tf_op jit(solution)/shard_map/all_to_all | solution.py:539
  153.0 30.9 %all_to_all.60.refs_1_.refs_2_.refs_10_.refs_11_ = f32[8,2,1,2,128,128]{5,4,3,2,1,0:T(8,128)} all-to-all(f32[8,2,1,2,128,128]{5,4,3,2,1,0:T(8,128)} %gate.13.refs_2_), channel_id=1, replica_groups=mesh['hel'=4,'rad'=8] {'rad'}, dimensions={0} | all-to-all | bytes 4194304 | tf_op jit(solution)/shard_map/all_to_all | solution.py:539
  203.1 35.5 %collective-permute-done.2.refs_4_ = f32[8,2,2,128,128]{4,3,2,1,0:T(8,128)} collective-permute-done((f32[8,2,2,128,128]{4,3,2,1,0:T(8,128)}, f32[8,2,2,128,128]{4,3,2,1,0:T(8,128)}, u32[]{:S(2)}, u32[]{:S(2)}) %collective-permute-start.2) | collective-permute-done | bytes 2097184 | tf_op jit(solution)/shard_map/ppermute | solution.py:544
  245.5 12.2 %shard_map.73 = (f32[8,2,2,128,128]{4,3,2,1,0:T(8,128)}, f32[8,2,2,128,128]{4,3,2,1,0:T(8,128)}) custom-call(s32[24,3]{1,0:T(8,128)} %copy.35.list_ref, f32[8,1,2,128,128]{4,3,2,1,0:T(8,128)} %get-tuple-element.84.refs_0_, f32[8,1,2,128,128]{4,3,2,1,0:T(8,128)} %get-tuple-element.85.refs_1_, ...), custom_call_target="tpu_custom_call" | custom-call | flops 3221225472 | bytes 16777216 | tf_op jit(solution)/shard_map/pallas_call | solution.py:480
  257.8 20.1 %kinetic.8.refs_0_ = f32[8,2,2,2,128,128]{5,4,3,2,1,0:T(8,128)} custom-call(f32[8,2,2,128,128]{4,3,2,1,0:T(8,128)} %get-tuple-element.46.refs_0_.refs_1_, f32[8,2,2,2,128,128]{5,4,3,2,1,0:T(8,128)} %all-to-all-done.4.refs_1_, bf16[4,2,256,1024]{3,2,1,0:T(8,128)(2,1)} %get-tuple-element.44.refs_2_, bf16[4,2,256,1024]{3,2,1,0:T(8,128)(2,1)} %get-tuple-element.45.refs_3_), custom_call_target="tpu_custom_call" | custom-call | flops 12884901888 | bytes 16777216 | tf_op jit(solution)/shard_map/kinetic/pallas_call | solution.py:251
  293.3 59.6 %collective-permute-done.4 = f32[8,1,2,128,128]{4,3,2,0,1:T(8,128)S(1)} collective-permute-done((f32[8,1,2,128,128]{4,3,2,0,1:T(8,128)}, f32[8,1,2,128,128]{4,3,2,0,1:T(8,128)S(1)}, u32[]{:S(2)}, u32[]{:S(2)}) %collective-permute-start.4) | collective-permute-done | bytes 1048608 | tf_op jit(solution)/shard_map/ppermute | solution.py:544
  367.3 14.2 %shard_map.75 = (f32[8,2,2,128,128]{4,3,2,1,0:T(8,128)}, f32[8,2,2,128,128]{4,3,2,1,0:T(8,128)}, f32[8,2,2,128,128]{4,3,2,1,0:T(8,128)}, f32[8,2,2,128,128]{4,3,2,1,0:T(8,128)}) custom-call(s32[24,3]{1,0:T(8,128)} %copy.35.list_ref, f32[8,1,2,128,128]{4,3,2,1,0:T(8,128)} %get-tuple-element.48.refs_0_.refs_2_, ...), custom_call_target="tpu_custom_call" | custom-call | flops 3221225472 | bytes 16777216 | tf_op jit(solution)/shard_map/pallas_call | solution.py:480
  394.5 16.8 %collective-permute-done.8.refs_4_ = f32[8,1,2,128,128]{4,3,2,1,0:T(8,128)S(1)} collective-permute-done((f32[8,1,2,128,128]{4,3,2,1,0:T(8,128)S(1)}, f32[8,1,2,128,128]{4,3,2,1,0:T(8,128)S(1)}, u32[]{:S(2)}, u32[]{:S(2)}) %collective-permute-start.8) | collective-permute-done | bytes 1048608 | tf_op jit(solution)/shard_map/ppermute | solution.py:544
  439.1 20.1 %kinetic.9.refs_0_ = f32[8,2,2,2,128,128]{5,4,3,2,1,0:T(8,128)} custom-call(f32[8,2,1,2,128,128]{5,4,3,2,1,0:T(8,128)} %gate.17.refs_0_, f32[8,2,2,2,128,128]{5,4,3,2,1,0:T(8,128)} %all-to-all-done.6.refs_1_, bf16[4,2,256,1024]{3,2,1,0:T(8,128)(2,1)} %get-tuple-element.44.refs_2_, bf16[4,2,256,1024]{3,2,1,0:T(8,128)(2,1)} %get-tuple-element.45.refs_3_), custom_call_target="tpu_custom_call" | custom-call | flops 12884901888 | bytes 16777216 | tf_op jit(solution)/shard_map/kinetic/pallas_call | solution.py:251
  483.2 36.9 %collective-permute-done.10.refs_3_ = f32[8,2,2,128,128]{4,3,2,1,0:T(8,128)} collective-permute-done((f32[8,2,2,128,128]{4,3,2,1,0:T(8,128)}, f32[8,2,2,128,128]{4,3,2,1,0:T(8,128)}, u32[]{:S(2)}, u32[]{:S(2)}) %collective-permute-start.10) | collective-permute-done | bytes 2097184 | tf_op jit(solution)/shard_map/ppermute | solution.py:544
  525.5 12.3 %shard_map.77 = (f32[8,2,2,128,128]{4,3,2,1,0:T(8,128)}, f32[8,2,2,128,128]{4,3,2,1,0:T(8,128)}) custom-call(s32[24,3]{1,0:T(8,128)} %copy.35.list_ref, f32[8,2,2,2,128,128]{5,4,3,2,1,0:T(8,128)} %gate.18.refs_0_, f32[8,2,2,2,128,128]{5,4,3,2,1,0:T(8,128)} %all-to-all-done.5.refs_1_.refs_2_.refs_10_.refs_11_, ...), custom_call_target="tpu_custom_call" | custom-call | flops 3221225472 | bytes 16777216 | tf_op jit(solution)/shard_map/pallas_call | solution.py:480
  556.7 12.4 %kinetic.10.refs_0_ = f32[8,2,1,2,128,128]{5,4,3,2,1,0:T(8,128)} custom-call(f32[2,8,1,2,128,128]{5,4,3,2,1,0:T(8,128)} %shard_map.78.refs_0_.refs_1_, f32[8,2,1,2,128,128]{5,4,3,2,1,0:T(8,128)} %copy-done.3, bf16[4,2,256,1024]{3,2,1,0:T(8,128)(2,1)} %get-tuple-element.44.refs_2_, bf16[4,2,256,1024]{3,2,1,0:T(8,128)(2,1)} %get-tuple-element.45.refs_3_), custom_call_target="tpu_custom_call" | custom-call | flops 6442450944 | bytes 12582912 | tf_op jit(solution)/shard_map/kinetic/pallas_call | solution.py:251
  587.2 27.2 %collective-permute-done.1 = f32[8,1,2,128,128]{4,3,2,0,1:T(8,128)S(1)} collective-permute-done((f32[8,1,2,128,128]{4,3,2,0,1:T(8,128)}, f32[8,1,2,128,128]{4,3,2,0,1:T(8,128)S(1)}, u32[]{:S(2)}, u32[]{:S(2)}) %collective-permute-start.1) | collective-permute-done | bytes 1048608 | tf_op jit(solution)/shard_map/ppermute | solution.py:545
  623.1 14.1 %shard_map.79 = (f32[8,2,2,128,128]{4,3,2,1,0:T(8,128)}, f32[8,2,2,128,128]{4,3,2,1,0:T(8,128)}, f32[8,2,2,128,128]{4,3,2,1,0:T(8,128)}, f32[8,2,2,128,128]{4,3,2,1,0:T(8,128)}) custom-call(s32[24,3]{1,0:T(8,128)} %copy.35.list_ref, f32[8,2,2,128,128]{4,3,2,1,0:T(8,128)} %get-tuple-element.78.refs_0_, f32[8,2,2,128,128]{4,3,2,1,0:T(8,128)} %get-tuple-element.77.refs_1_, ...), custom_call_target="tpu_custom_call" | custom-call | flops 3221225472 | bytes 16777216 | tf_op jit(solution)/shard_map/pallas_call | solution.py:480
  645.1 9.8 %collective-permute-done.16.refs_3_ = f32[8,2,2,128,128]{4,3,2,1,0:T(8,128)} collective-permute-done((f32[8,2,2,128,128]{4,3,2,1,0:T(8,128)}, f32[8,2,2,128,128]{4,3,2,1,0:T(8,128)}, u32[]{:S(2)}, u32[]{:S(2)}) %collective-permute-start.16) | collective-permute-done | bytes 2097184 | tf_op jit(solution)/shard_map/ppermute | solution.py:544
  665.1 12.2 %shard_map.80 = (f32[8,2,2,128,128]{4,3,2,1,0:T(8,128)}, f32[8,2,2,128,128]{4,3,2,1,0:T(8,128)}) custom-call(s32[24,3]{1,0:T(8,128)} %copy.35.list_ref, f32[8,2,1,2,128,128]{5,4,3,2,1,0:T(8,128)} %gate.20.refs_0_, f32[8,2,2,2,128,128]{5,4,3,2,1,0:T(8,128)} %all-to-all-done.8.refs_1_.refs_2_.refs_9_.refs_10_, ...), custom_call_target="tpu_custom_call" | custom-call | flops 3221225472 | bytes 16777216 | tf_op jit(solution)/shard_map/pallas_call | solution.py:480
  680.2 19.6 %collective-permute-done.18.refs_3_ = f32[8,2,2,128,128]{4,3,2,1,0:T(8,128)} collective-permute-done((f32[8,2,2,128,128]{4,3,2,1,0:T(8,128)}, f32[8,2,2,128,128]{4,3,2,1,0:T(8,128)}, u32[]{:S(2)}, u32[]{:S(2)}) %collective-permute-start.18) | collective-permute-done | bytes 2097184 | tf_op jit(solution)/shard_map/ppermute | solution.py:544
  702.4 12.4 %kinetic.11.refs_0_ = f32[8,2,1,2,128,128]{5,4,3,2,1,0:T(8,128)} custom-call(f32[8,2,2,128,128]{4,3,2,1,0:T(8,128)} %get-tuple-element.59.refs_0_.refs_1_, f32[8,2,1,2,128,128]{5,4,3,2,1,0:T(8,128)} %copy-done.4, bf16[4,2,256,1024]{3,2,1,0:T(8,128)(2,1)} %get-tuple-element.44.refs_2_, bf16[4,2,256,1024]{3,2,1,0:T(8,128)(2,1)} %get-tuple-element.45.refs_3_), custom_call_target="tpu_custom_call" | custom-call | flops 6442450944 | bytes 12582912 | tf_op jit(solution)/shard_map/kinetic/pallas_call | solution.py:251
  719.0 13.1 %shard_map.81.refs_0_ = f32[2,8,2,2,128,128]{5,4,3,2,1,0:T(8,128)} custom-call(s32[24,3]{1,0:T(8,128)} %copy.35.list_ref, f32[8,2,1,2,128,128]{5,4,3,2,1,0:T(8,128)} %gate.21.refs_0_, f32[8,2,2,128,128]{4,3,2,1,0:T(8,128)} %get-tuple-element.50.refs_2_.refs_1_, f32[8,2,2,128,128]{4,3,2,1,0:T(8,128)} %get-tuple-element.60.refs_2_, ...), custom_call_target="tpu_custom_call" | custom-call | flops 3221225472 | bytes 16777216 | tf_op jit(solution)/shard_map/pallas_call | solution.py:480
  732.1 12.7 %collective-permute-done.20.refs_3_ = f32[8,2,2,128,128]{4,3,2,1,0:T(8,128)} collective-permute-done((f32[8,2,2,128,128]{4,3,2,1,0:T(8,128)}, f32[8,2,2,128,128]{4,3,2,1,0:T(8,128)}, u32[]{:S(2)}, u32[]{:S(2)}) %collective-permute-start.20) | collective-permute-done | bytes 2097184 | tf_op jit(solution)/shard_map/ppermute | solution.py:544
  744.8 10.3 %collective-permute-done.21.refs_4_ = f32[8,2,2,128,128]{4,3,2,1,0:T(8,128)} collective-permute-done((f32[8,2,2,128,128]{4,3,2,1,0:T(8,128)}, f32[8,2,2,128,128]{4,3,2,1,0:T(8,128)}, u32[]{:S(2)}, u32[]{:S(2)}) %collective-permute-start.21) | collective-permute-done | bytes 2097184 | tf_op jit(solution)/shard_map/ppermute | solution.py:545
  755.0 13.2 %shard_map.82.refs_0_.refs_2_ = f32[2,8,2,2,128,128]{5,4,3,2,1,0:T(8,128)} custom-call(s32[24,3]{1,0:T(8,128)} %copy.35.list_ref, f32[2,8,2,2,128,128]{5,4,3,2,1,0:T(8,128)} %shard_map.81.refs_0_, f32[8,2,2,128,128]{4,3,2,1,0:T(8,128)} %get-tuple-element.58.refs_2_.refs_1_, f32[8,2,2,128,128]{4,3,2,1,0:T(8,128)} %get-tuple-element.63.refs_2_, ...), custom_call_target="tpu_custom_call" | custom-call | flops 3221225472 | bytes 16777216 | tf_op jit(solution)/shard_map/pallas_call | solution.py:480
  777.8 11.3 %collective-permute-done.22.refs_3_ = f32[8,2,2,128,128]{4,3,2,1,0:T(8,128)} collective-permute-done((f32[8,2,2,128,128]{4,3,2,1,0:T(8,128)}, f32[8,2,2,128,128]{4,3,2,1,0:T(8,128)}, u32[]{:S(2)}, u32[]{:S(2)}) %collective-permute-start.22) | collective-permute-done | bytes 2097184 | tf_op jit(solution)/shard_map/ppermute | solution.py:544
  798.2 14.3 %shard_map.84 = (f32[8,2,2,128,128]{4,3,2,1,0:T(8,128)}, f32[8,2,2,128,128]{4,3,2,1,0:T(8,128)}, f32[8,2,2,128,128]{4,3,2,1,0:T(8,128)}, f32[8,2,2,128,128]{4,3,2,1,0:T(8,128)}) custom-call(s32[24,3]{1,0:T(8,128)} %copy.35.list_ref, f32[8,1,2,128,128]{4,3,2,1,0:T(8,128)} %get-tuple-element.66.refs_0_.refs_1_, ...), custom_call_target="tpu_custom_call" | custom-call | flops 3221225472 | bytes 16777216 | tf_op jit(solution)/shard_map/pallas_call | solution.py:480
  822.5 57.7 %collective-permute-done.24.refs_3_ = f32[8,1,2,128,128]{4,3,2,1,0:T(8,128)} collective-permute-done((f32[8,1,2,128,128]{4,3,2,1,0:T(8,128)}, f32[8,1,2,128,128]{4,3,2,1,0:T(8,128)}, u32[]{:S(2)}, u32[]{:S(2)}) %collective-permute-start.24) | collective-permute-done | bytes 1048608 | tf_op jit(solution)/shard_map/ppermute | solution.py:544
  898.9 13.1 %shard_map.86.refs_0_.refs_3_ = f32[2,8,2,2,128,128]{5,4,3,2,1,0:T(8,128)} custom-call(s32[24,3]{1,0:T(8,128)} %copy.35.list_ref, f32[8,1,2,128,128]{4,3,2,1,0:T(8,128)} %get-tuple-element.70.refs_0_.refs_1_, f32[8,2,2,128,128]{4,3,2,1,0:T(8,128)} %get-tuple-element.68.refs_0_.refs_1_, f32[8,2,2,128,128]{4,3,2,1,0:T(8,128)} %get-tuple-element.71.refs_2_, ...), custom_call_target="tpu_custom_call" | custom-call | flops 3221225472 | bytes 16777216 | tf_op jit(solution)/shard_map/pallas_call | solution.py:480
  929.6 12.4 %unpack.1 = f32[2,2,128,8,1024]{4,3,2,1,0:T(8,128)} custom-call(f32[2,8,2,2,128,128]{5,4,3,2,1,0:T(8,128)} %shard_map.81.refs_0_, f32[2,8,1,2,128,128]{5,4,3,2,1,0:T(8,128)} %shard_map.78.refs_0_.refs_1_, f32[2,8,2,2,128,128]{5,4,3,2,1,0:T(8,128)} %shard_map.82.refs_0_.refs_2_, f32[2,8,2,2,128,128]{5,4,3,2,1,0:T(8,128)} %shard_map.86.refs_0_.refs_3_, ...), custom_call_target="tpu_custom_call" | custom-call | tf_op jit(solution)/shard_map/unpack/pallas_call | solution.py:325
  (147 shorter events, 302.7 us)
Async XLA Ops:
  8.7 54.4 %all-to-all-start = ((f32[8,2,2,2,128,128]{5,4,3,2,1,0:T(8,128)}), f32[8,2,2,2,128,128]{5,4,3,2,1,0:T(8,128)}, u32[]{:S(2)}, u32[]{:S(2)}) async-start(f32[8,2,2,2,128,128]{5,4,3,2,1,0:T(8,128)} %pack.3), calls=%async_computation | async-start | bytes 8388608 | tf_op jit(solution)/shard_map/all_to_all | solution.py:539
  94.5 53.7 %all-to-all-start.2 = ((f32[8,2,2,2,128,128]{5,4,3,2,1,0:T(8,128)}), f32[8,2,2,2,128,128]{5,4,3,2,1,0:T(8,128)}, u32[]{:S(2)}, u32[]{:S(2)}) async-start(f32[8,2,2,2,128,128]{5,4,3,2,1,0:T(8,128)} %gate.12.refs_0_), calls=%async_computation.2 | async-start | bytes 8388608 | tf_op jit(solution)/shard_map/all_to_all | solution.py:539
  183.9 73.8 %all-to-all-start.4 = ((f32[8,2,2,2,128,128]{5,4,3,2,1,0:T(8,128)}), f32[8,2,2,2,128,128]{5,4,3,2,1,0:T(8,128)}, u32[]{:S(2)}, u32[]{:S(2)}) async-start(f32[8,2,2,2,128,128]{5,4,3,2,1,0:T(8,128)} %gate.14), calls=%async_computation.4 | async-start | bytes 8388608 | tf_op jit(solution)/shard_map/all_to_all | solution.py:539
  188.6 49.9 %collective-permute-start.2 = (f32[8,2,2,128,128]{4,3,2,1,0:T(8,128)}, f32[8,2,2,128,128]{4,3,2,1,0:T(8,128)}, u32[]{:S(2)}, u32[]{:S(2)}) collective-permute-start(f32[8,2,2,128,128]{4,3,2,1,0:T(8,128)} %get-tuple-element.81.refs_3_), channel_id=1, source_target_pairs={{0,8},{8,16},{16,24},{1,9},{9,17},{17,25},{2,10},{10,18},{18,26},{... | collective-permute-start | bytes 6291464 | tf_op jit(solution)/shard_map/ppermute | solution.py:544
  194.2 49.6 %collective-permute-start.3 = (f32[8,2,2,128,128]{4,3,2,1,0:T(8,128)S(1)}, f32[8,2,2,128,128]{4,3,2,1,0:T(8,128)}, u32[]{:S(2)}, u32[]{:S(2)}) collective-permute-start(f32[8,2,2,128,128]{4,3,2,1,0:T(8,128)S(1)} %copy-done.7), channel_id=1, source_target_pairs={{8,0},{16,8},{24,16},{9,1},{17,9},{25,17},{10,2},{18,10},{26,18},{... | collective-permute-start | bytes 6291464 | tf_op jit(solution)/shard_map/ppermute | solution.py:545
  277.8 103.6 %all-to-all-start.5 = ((f32[8,2,2,2,128,128]{5,4,3,2,1,0:T(8,128)}), f32[8,2,2,2,128,128]{5,4,3,2,1,0:T(8,128)}, u32[]{:S(2)}, u32[]{:S(2)}) async-start(f32[8,2,2,2,128,128]{5,4,3,2,1,0:T(8,128)} %gate.15.refs_0_), calls=%async_computation.5 | async-start | bytes 8388608 | tf_op jit(solution)/shard_map/all_to_all | solution.py:539
  282.5 84.8 %collective-permute-start.6 = (f32[8,2,2,128,128]{4,3,2,1,0:T(8,128)}, f32[8,2,2,128,128]{4,3,2,1,0:T(8,128)}, u32[]{:S(2)}, u32[]{:S(2)}) collective-permute-start(f32[8,2,2,128,128]{4,3,2,1,0:T(8,128)} %get-tuple-element.49.refs_2_), channel_id=1, source_target_pairs={{0,8},{8,16},{16,24},{1,9},{9,17},{17,25},{2,10},{10,18},{18,26},{... | collective-permute-start | bytes 6291464 | tf_op jit(solution)/shard_map/ppermute | solution.py:544
  286.0 81.2 %collective-permute-start.7 = (f32[8,2,2,128,128]{4,3,2,1,0:T(8,128)S(1)}, f32[8,2,2,128,128]{4,3,2,1,0:T(8,128)}, u32[]{:S(2)}, u32[]{:S(2)}) collective-permute-start(f32[8,2,2,128,128]{4,3,2,1,0:T(8,128)S(1)} %copy-done.11), channel_id=1, source_target_pairs={{8,0},{16,8},{24,16},{9,1},{17,9},{25,17},{10,2},{18,10},{26,18},{... | collective-permute-start | bytes 6291464 | tf_op jit(solution)/shard_map/ppermute | solution.py:545
  287.3 65.5 %collective-permute-start.4 = (f32[8,1,2,128,128]{4,3,2,0,1:T(8,128)}, f32[8,1,2,128,128]{4,3,2,0,1:T(8,128)S(1)}, u32[]{:S(2)}, u32[]{:S(2)}) collective-permute-start(f32[8,1,2,128,128]{4,3,2,0,1:T(8,128)} %get-tuple-element.86), channel_id=1, source_target_pairs={{0,8},{8,16},{16,24},{1,9},{9,17},{17,25},{2,10},{10,18},{18,26},{... | collective-permute-start | bytes 3145736 | tf_op jit(solution)/shard_map/ppermute | solution.py:544
  292.0 66.1 %collective-permute-start.5 = (f32[8,1,2,128,128]{4,3,2,0,1:T(8,128)S(1)}, f32[8,1,2,128,128]{4,3,2,0,1:T(8,128)S(1)}, u32[]{:S(2)}, u32[]{:S(2)}) collective-permute-start(f32[8,1,2,128,128]{4,3,2,0,1:T(8,128)S(1)} %get-tuple-element.83), channel_id=1, source_target_pairs={{8,0},{16,8},{24,16},{9,1},{17,9},{25,17},{10,2},{18,10},{26,18},{... | collective-permute-start | bytes 3145736 | tf_op jit(solution)/shard_map/ppermute | solution.py:545
  381.5 53.8 %all-to-all-start.6 = ((f32[8,2,2,2,128,128]{5,4,3,2,1,0:T(8,128)}), f32[8,2,2,2,128,128]{5,4,3,2,1,0:T(8,128)}, u32[]{:S(2)}, u32[]{:S(2)}) async-start(f32[8,2,2,2,128,128]{5,4,3,2,1,0:T(8,128)} %gate.16), calls=%async_computation.6 | async-start | bytes 8388608 | tf_op jit(solution)/shard_map/all_to_all | solution.py:539
  466.8 102.4 %all-to-all-start.8 = ((f32[8,2,2,2,128,128]{5,4,3,2,1,0:T(8,128)}), f32[8,2,2,2,128,128]{5,4,3,2,1,0:T(8,128)}, u32[]{:S(2)}, u32[]{:S(2)}) async-start(f32[8,2,2,2,128,128]{5,4,3,2,1,0:T(8,128)} %gate.18.refs_0_), calls=%async_computation.8 | async-start | bytes 8388608 | tf_op jit(solution)/shard_map/all_to_all | solution.py:539
  475.1 50.5 %collective-permute-start.11 = (f32[8,2,2,128,128]{4,3,2,1,0:T(8,128)S(1)}, f32[8,2,2,128,128]{4,3,2,1,0:T(8,128)}, u32[]{:S(2)}, u32[]{:S(2)}) collective-permute-start(f32[8,2,2,128,128]{4,3,2,1,0:T(8,128)S(1)} %copy-done.6), channel_id=1, source_target_pairs={{8,0},{16,8},{24,16},{9,1},{17,9},{25,17},{10,2},{18,10},{26,18},{... | collective-permute-start | bytes 6291464 | tf_op jit(solution)/shard_map/ppermute | solution.py:545
  476.3 66.2 %collective-permute-start.12 = (f32[8,1,2,128,128]{4,3,2,1,0:T(8,128)}, f32[8,1,2,128,128]{4,3,2,1,0:T(8,128)}, u32[]{:S(2)}, u32[]{:S(2)}) collective-permute-start(f32[8,1,2,128,128]{4,3,2,1,0:T(8,128)} %get-tuple-element.54.refs_2_), channel_id=1, source_target_pairs={{0,8},{8,16},{16,24},{1,9},{9,17},{17,25},{2,10},{10,18},{18,26},{... | collective-permute-start | bytes 3145736 | tf_op jit(solution)/shard_map/ppermute | solution.py:544
  481.9 66.1 %collective-permute-start.13 = (f32[8,1,2,128,128]{4,3,2,1,0:T(8,128)S(1)}, f32[8,1,2,128,128]{4,3,2,1,0:T(8,128)}, u32[]{:S(2)}, u32[]{:S(2)}) collective-permute-start(f32[8,1,2,128,128]{4,3,2,1,0:T(8,128)S(1)} %copy-done.9), channel_id=1, source_target_pairs={{8,0},{16,8},{24,16},{9,1},{17,9},{25,17},{10,2},{18,10},{26,18},{... | collective-permute-start | bytes 3145736 | tf_op jit(solution)/shard_map/ppermute | solution.py:545
  537.8 85.3 %collective-permute-start.14 = (f32[8,2,2,128,128]{4,3,2,1,0:T(8,128)}, f32[8,2,2,128,128]{4,3,2,1,0:T(8,128)}, u32[]{:S(2)}, u32[]{:S(2)}) collective-permute-start(f32[8,2,2,128,128]{4,3,2,1,0:T(8,128)} %get-tuple-element.57.refs_3_), channel_id=1, source_target_pairs={{0,8},{8,16},{16,24},{1,9},{9,17},{17,25},{2,10},{10,18},{18,26},{... | collective-permute-start | bytes 6291464 | tf_op jit(solution)/shard_map/ppermute | solution.py:544
  540.5 82.7 %collective-permute-start.15 = (f32[8,2,2,128,128]{4,3,2,1,0:T(8,128)}, f32[8,2,2,128,128]{4,3,2,1,0:T(8,128)}, u32[]{:S(2)}, u32[]{:S(2)}) collective-permute-start(f32[8,2,2,128,128]{4,3,2,1,0:T(8,128)} %get-tuple-element.53.refs_0_.refs_2_), channel_id=1, source_target_pairs={{8,0},{16,8},{24,16},{9,1},{17,9},{25,17},{10,2},{18,10},{26,18},{... | collective-permute-start | bytes 6291464 | tf_op jit(solution)/shard_map/ppermute | solution.py:545
  569.1 68.1 %all-to-all-start.9 = ((f32[8,2,1,2,128,128]{5,4,3,2,1,0:T(8,128)}), f32[8,2,1,2,128,128]{5,4,3,2,1,0:T(8,128)S(1)}, u32[]{:S(2)}, u32[]{:S(2)}) async-start(f32[8,2,1,2,128,128]{5,4,3,2,1,0:T(8,128)} %gate.19), calls=%async_computation.9 | async-start | bytes 4194304 | tf_op jit(solution)/shard_map/all_to_all | solution.py:539
  584.0 70.9 %collective-permute-start.16 = (f32[8,2,2,128,128]{4,3,2,1,0:T(8,128)}, f32[8,2,2,128,128]{4,3,2,1,0:T(8,128)}, u32[]{:S(2)}, u32[]{:S(2)}) collective-permute-start(f32[8,2,2,128,128]{4,3,2,1,0:T(8,128)} %get-tuple-element.77.refs_1_), channel_id=1, source_target_pairs={{0,8},{8,16},{16,24},{1,9},{9,17},{17,25},{2,10},{10,18},{18,26},{... | collective-permute-start | bytes 6291464 | tf_op jit(solution)/shard_map/ppermute | solution.py:544
  614.4 50.7 %collective-permute-start.17 = (f32[8,2,2,128,128]{4,3,2,1,0:T(8,128)}, f32[8,2,2,128,128]{4,3,2,1,0:T(8,128)}, u32[]{:S(2)}, u32[]{:S(2)}) collective-permute-start(f32[8,2,2,128,128]{4,3,2,1,0:T(8,128)} %get-tuple-element.78.refs_0_), channel_id=1, source_target_pairs={{8,0},{16,8},{24,16},{9,1},{17,9},{25,17},{10,2},{18,10},{26,18},{... | collective-permute-start | bytes 6291464 | tf_op jit(solution)/shard_map/ppermute | solution.py:545
  617.2 82.6 %collective-permute-start.18 = (f32[8,2,2,128,128]{4,3,2,1,0:T(8,128)}, f32[8,2,2,128,128]{4,3,2,1,0:T(8,128)}, u32[]{:S(2)}, u32[]{:S(2)}) collective-permute-start(f32[8,2,2,128,128]{4,3,2,1,0:T(8,128)} %get-tuple-element.60.refs_2_), channel_id=1, source_target_pairs={{0,8},{8,16},{16,24},{1,9},{9,17},{17,25},{2,10},{10,18},{18,26},{... | collective-permute-start | bytes 6291464 | tf_op jit(solution)/shard_map/ppermute | solution.py:544
  638.6 62.5 %all-to-all-start.10 = ((f32[8,2,1,2,128,128]{5,4,3,2,1,0:T(8,128)}), f32[8,2,1,2,128,128]{5,4,3,2,1,0:T(8,128)S(1)}, u32[]{:S(2)}, u32[]{:S(2)}) async-start(f32[8,2,1,2,128,128]{5,4,3,2,1,0:T(8,128)} %gate.20.refs_0_), calls=%async_computation.10 | async-start | bytes 4194304 | tf_op jit(solution)/shard_map/all_to_all | solution.py:539
  642.5 76.5 %collective-permute-start.19 = (f32[8,2,2,128,128]{4,3,2,1,0:T(8,128)}, f32[8,2,2,128,128]{4,3,2,1,0:T(8,128)}, u32[]{:S(2)}, u32[]{:S(2)}) collective-permute-start(f32[8,2,2,128,128]{4,3,2,1,0:T(8,128)} %get-tuple-element.50.refs_2_.refs_1_), channel_id=1, source_target_pairs={{8,0},{16,8},{24,16},{9,1},{17,9},{25,17},{10,2},{18,10},{26,18},{... | collective-permute-start | bytes 6291464 | tf_op jit(solution)/shard_map/ppermute | solution.py:545
  643.8 111.2 %collective-permute-start.21 = (f32[8,2,2,128,128]{4,3,2,1,0:T(8,128)}, f32[8,2,2,128,128]{4,3,2,1,0:T(8,128)}, u32[]{:S(2)}, u32[]{:S(2)}) collective-permute-start(f32[8,2,2,128,128]{4,3,2,1,0:T(8,128)} %get-tuple-element.58.refs_2_.refs_1_), channel_id=1, source_target_pairs={{8,0},{16,8},{24,16},{9,1},{17,9},{25,17},{10,2},{18,10},{26,18},{... | collective-permute-start | bytes 6291464 | tf_op jit(solution)/shard_map/ppermute | solution.py:545
  654.9 89.9 %collective-permute-start.20 = (f32[8,2,2,128,128]{4,3,2,1,0:T(8,128)}, f32[8,2,2,128,128]{4,3,2,1,0:T(8,128)}, u32[]{:S(2)}, u32[]{:S(2)}) collective-permute-start(f32[8,2,2,128,128]{4,3,2,1,0:T(8,128)} %get-tuple-element.63.refs_2_), channel_id=1, source_target_pairs={{0,8},{8,16},{16,24},{1,9},{9,17},{17,25},{2,10},{10,18},{18,26},{... | collective-permute-start | bytes 6291464 | tf_op jit(solution)/shard_map/ppermute | solution.py:544
  677.4 111.7 %collective-permute-start.22 = (f32[8,2,2,128,128]{4,3,2,1,0:T(8,128)}, f32[8,2,2,128,128]{4,3,2,1,0:T(8,128)}, u32[]{:S(2)}, u32[]{:S(2)}) collective-permute-start(f32[8,2,2,128,128]{4,3,2,1,0:T(8,128)} %get-tuple-element.67.refs_2_), channel_id=1, source_target_pairs={{0,8},{8,16},{16,24},{1,9},{9,17},{17,25},{2,10},{10,18},{18,26},{... | collective-permute-start | bytes 6291464 | tf_op jit(solution)/shard_map/ppermute | solution.py:544
  699.8 98.4 %collective-permute-start.23 = (f32[8,2,2,128,128]{4,3,2,1,0:T(8,128)}, f32[8,2,2,128,128]{4,3,2,1,0:T(8,128)}, u32[]{:S(2)}, u32[]{:S(2)}) collective-permute-start(f32[8,2,2,128,128]{4,3,2,1,0:T(8,128)} %get-tuple-element.59.refs_0_.refs_1_), channel_id=1, source_target_pairs={{8,0},{16,8},{24,16},{9,1},{17,9},{25,17},{10,2},{18,10},{26,18},{... | collective-permute-start | bytes 6291464 | tf_op jit(solution)/shard_map/ppermute | solution.py:545
  714.9 53.3 %all-to-all-start.11 = ((f32[8,2,1,2,128,128]{5,4,3,2,1,0:T(8,128)}), f32[8,2,1,2,128,128]{5,4,3,2,1,0:T(8,128)S(1)}, u32[]{:S(2)}, u32[]{:S(2)}) async-start(f32[8,2,1,2,128,128]{5,4,3,2,1,0:T(8,128)} %gate.21.refs_0_), calls=%async_computation.11 | async-start | bytes 4194304 | tf_op jit(solution)/shard_map/all_to_all | solution.py:539
  812.5 85.1 %collective-permute-start.26 = (f32[8,2,2,128,128]{4,3,2,1,0:T(8,128)}, f32[8,2,2,128,128]{4,3,2,1,0:T(8,128)S(1)}, u32[]{:S(2)}, u32[]{:S(2)}) collective-permute-start(f32[8,2,2,128,128]{4,3,2,1,0:T(8,128)} %get-tuple-element.71.refs_2_), channel_id=1, source_target_pairs={{0,8},{8,16},{16,24},{1,9},{9,17},{17,25},{2,10},{10,18},{18,26},{... | collective-permute-start | bytes 6291464 | tf_op jit(solution)/shard_map/ppermute | solution.py:544
  814.4 83.2 %collective-permute-start.27 = (f32[8,2,2,128,128]{4,3,2,1,0:T(8,128)}, f32[8,2,2,128,128]{4,3,2,1,0:T(8,128)}, u32[]{:S(2)}, u32[]{:S(2)}) collective-permute-start(f32[8,2,2,128,128]{4,3,2,1,0:T(8,128)} %get-tuple-element.68.refs_0_.refs_1_), channel_id=1, source_target_pairs={{8,0},{16,8},{24,16},{9,1},{17,9},{25,17},{10,2},{18,10},{26,18},{... | collective-permute-start | bytes 6291464 | tf_op jit(solution)/shard_map/ppermute | solution.py:545
  815.7 64.6 %collective-permute-start.24 = (f32[8,1,2,128,128]{4,3,2,1,0:T(8,128)}, f32[8,1,2,128,128]{4,3,2,1,0:T(8,128)}, u32[]{:S(2)}, u32[]{:S(2)}) collective-permute-start(f32[8,1,2,128,128]{4,3,2,1,0:T(8,128)} %get-tuple-element.69.refs_2_), channel_id=1, source_target_pairs={{0,8},{8,16},{16,24},{1,9},{9,17},{17,25},{2,10},{10,18},{18,26},{... | collective-permute-start | bytes 3145736 | tf_op jit(solution)/shard_map/ppermute | solution.py:544
  821.3 63.5 %collective-permute-start.25 = (f32[8,1,2,128,128]{4,3,2,1,0:T(8,128)S(1)}, f32[8,1,2,128,128]{4,3,2,1,0:T(8,128)}, u32[]{:S(2)}, u32[]{:S(2)}) collective-permute-start(f32[8,1,2,128,128]{4,3,2,1,0:T(8,128)S(1)} %copy-done.10), channel_id=1, source_target_pairs={{8,0},{16,8},{24,16},{9,1},{17,9},{25,17},{10,2},{18,10},{26,18},{... | collective-permute-start | bytes 3145736 | tf_op jit(solution)/shard_map/ppermute | solution.py:545
  (32 other events, 465.9 us)
